TPU v7x, 256 devices: a whole 4x4x8 slice. The times are simulated.
256 devices in a mesh: dp: 64 (over y, z, core), mp: 4 (over x).
Axes of the slice: x: 4, y: 4, z: 8, core: 2. Of those that a mesh axis runs over, the one named last changes fastest.
Arguments:
- seg_queries: bfloat16 [64, 256, 3072], P('dp', None, 'mp'), may hold values from -6 to 6
- seg_keys: bfloat16 [64, 256, 3072], P('dp', None, 'mp'), may hold values from -6 to 6
- seg_values: bfloat16 [64, 256, 3072], P('dp', None, 'mp'), may hold values from -8 to 8
- memory_keys: bfloat16 [64, 256, 3072], P('dp', None, 'mp'), may hold values from -4 to 4
- memory_values: bfloat16 [64, 256, 3072], P('dp', None, 'mp'), may hold values from -8 to 8
- new_owner: int32 [64], replicated, may hold values from 0 to 63, each once
- kept_blocks: int32 [64], replicated, may hold values from 1 to 2, 96 in all
- rel_bias: float32 [24, 512], P('mp'), may hold values from -5 to 5
- norm_gain: float32 [3072], P('mp'), may hold values from 0.5 to 1.5
- cotangent: bfloat16 [64, 256, 3072], P('dp', None, 'mp'), may hold values from -8 to 8
Outputs:
- attended: bfloat16 [64, 256, 3072], P('dp', None, 'mp')
- query_grad: bfloat16 [64, 256, 3072], P('dp', None, 'mp')
- key_grad: bfloat16 [64, 256, 3072], P('dp', None, 'mp')
- value_grad: bfloat16 [64, 256, 3072], P('dp', None, 'mp')
- bias_grad: float32 [24, 512], P('mp', 'dp')
- gain_grad: float32 [3072], P('mp')
Inputs may be any that keep to these rules, and one draw needn't show every extreme that they name: `new_owner`: each old slot's stream goes to one device, and every device takes exactly one stream. A slot keeps its most recent kept_blocks blocks of 128 memory positions; some slot keeps all 2.
All inputs are finite; a program needn't handle non-finite values.
Results may differ from a plain program's by a relative error of at most 0.018.
Values may be sent and summed in bfloat16 or wider, within the bound.
No kernel may reach another device: no remote copies, remote signals or barrier semaphores. Data moves between devices by JAX's collectives and lax.ppermute only.
A program may use at most 64 MiB of HBM per device.

v0:
```python
import math

import jax
import jax.numpy as jnp
from jax import lax
from jax.experimental import pallas as pl
from jax.experimental.pallas import tpu as pltpu
from jax.sharding import PartitionSpec as P

DH = 128
BLOCK = 128
HD = 3072
SEG = 256
MEM = 256
POS = 512
HEADS = 6
COLS = HEADS * DH
DP = 64
PIECE = (2 * MEM) // DP
LOG2E = math.log2(math.e)
SCALE = DH ** (-0.5)
NT = (((1,), (1,)), ((), ()))
NN = (((1,), (0,)), ((), ()))
TN = (((0,), (0,)), ((), ()))


def dot(a, b, dims):
    return lax.dot_general(a, b, dims, preferred_element_type=jnp.float32)


def roll(x, shift):
    shift = shift % x.shape[1]
    return x if shift == 0 else pltpu.roll(x, shift, axis=1)


def reverse_lanes(x):
    rows, width = x.shape
    index = 127 - lax.broadcasted_iota(jnp.int32, (rows, 128), 1)
    parts = [
        jnp.take_along_axis(x[:, start : start + 128], index, axis=1)
        for start in range(width - 128, -1, -128)
    ]
    return jnp.concatenate(parts, axis=1)


def by_distance(x):
    return roll(reverse_lanes(x), -255)


def stagger(x, unit):
    row = lax.broadcasted_iota(jnp.int32, x.shape, 0)
    for bit in (1, 2, 4):
        x = jnp.where((row & bit) != 0, roll(x, bit * unit), x)
    return x


def bias_rows(table_row):
    base = stagger(jnp.broadcast_to(by_distance(jnp.broadcast_to(table_row, (8, POS))), (8, POS)), 1)
    return jnp.concatenate([roll(base, 8 * group) for group in range(SEG // 8)], axis=0)


def diagonal_row(score_grad):
    level = [score_grad[8 * g : 8 * g + 8] for g in range(SEG // 8)]
    shift = 8
    while len(level) > 1:
        level = [level[k] + roll(level[k + 1], -shift) for k in range(0, len(level), 2)]
        shift *= 2
    return jnp.sum(stagger(level[0], -1), axis=0, keepdims=True)


def reorder_kernel(owner_ref, in_ref, out_ref):
    for slot in range(DP):
        out_ref[owner_ref[slot]] = in_ref[slot]


def reorder(new_owner, pieces):
    return pl.pallas_call(
        reorder_kernel,
        out_shape=jax.ShapeDtypeStruct(pieces.shape, pieces.dtype),
        in_specs=[
            pl.BlockSpec(memory_space=pltpu.SMEM),
            pl.BlockSpec(memory_space=pltpu.VMEM),
        ],
        out_specs=pl.BlockSpec(memory_space=pltpu.VMEM),
        name="reorder",
    )(new_owner, pieces)


def forward_kernel(
    kept_ref, q_ref, ks_ref, vs_ref, mem_ref, bias_ref, cot_ref, gain_ref,
    out_ref, prob_ref, stats_ref, square_ref, cross_ref,
):
    head = pl.program_id(0)
    q = q_ref[0]
    bias = bias_rows(bias_ref[pl.ds(head, 1), :] * LOG2E)
    factor = SCALE * LOG2E
    s_mem = dot(q, mem_ref[:MEM], NT) * factor + bias[:, :MEM]
    s_seg = dot(q, ks_ref[0], NT) * factor + bias[:, MEM:]
    col = lax.broadcasted_iota(jnp.int32, (SEG, MEM), 1)
    row = lax.broadcasted_iota(jnp.int32, (SEG, MEM), 0)
    s_mem = jnp.where(col >= MEM - BLOCK * kept_ref[0], s_mem, -1e30)
    s_seg = jnp.where(col <= row, s_seg, -1e30)
    top = jnp.maximum(
        jnp.max(s_mem, axis=1, keepdims=True), jnp.max(s_seg, axis=1, keepdims=True)
    )
    p_mem = jnp.exp2(s_mem - top)
    p_seg = jnp.exp2(s_seg - top)
    total = jnp.sum(p_mem, axis=1, keepdims=True) + jnp.sum(p_seg, axis=1, keepdims=True)
    inverse = 1.0 / total
    w_mem = (p_mem * inverse).astype(jnp.bfloat16)
    w_seg = (p_seg * inverse).astype(jnp.bfloat16)
    prob_ref[0, :, :MEM] = w_mem
    prob_ref[0, :, MEM:] = w_seg
    out = dot(w_mem, mem_ref[MEM:], NN) + dot(w_seg, vs_ref[0], NN)
    out_ref[...] = out
    square = out * out
    cross = cot_ref[0].astype(jnp.float32) * gain_ref[...] * out

    @pl.when(head == 0)
    def _():
        square_ref[...] = square
        cross_ref[...] = cross

    @pl.when(head > 0)
    def _():
        square_ref[...] += square
        cross_ref[...] += cross

    @pl.when(head == HEADS - 1)
    def _():
        stats_ref[...] = jnp.zeros((8, SEG), jnp.float32)
        stats_ref[0:1, :] = jnp.sum(square_ref[...].T, axis=0, keepdims=True)
        stats_ref[1:2, :] = jnp.sum(cross_ref[...].T, axis=0, keepdims=True)


def column_spec():
    return pl.BlockSpec((1, SEG, DH), lambda h: (0, 0, h))


def whole(shape):
    return pl.BlockSpec(shape, lambda h: (0,) * len(shape))


def forward(kept, q, ks, vs, mem, bias, cot, gain):
    return pl.pallas_call(
        forward_kernel,
        grid=(HEADS,),
        out_shape=(
            jax.ShapeDtypeStruct((SEG, COLS), jnp.float32),
            jax.ShapeDtypeStruct((HEADS, SEG, POS), jnp.bfloat16),
            jax.ShapeDtypeStruct((8, SEG), jnp.float32),
        ),
        in_specs=[
            pl.BlockSpec(memory_space=pltpu.SMEM),
            column_spec(),
            column_spec(),
            column_spec(),
            pl.BlockSpec((2 * MEM, DH), lambda h: (0, h)),
            whole((HEADS, POS)),
            column_spec(),
            pl.BlockSpec((1, DH), lambda h: (0, h)),
        ],
        out_specs=(
            pl.BlockSpec((SEG, DH), lambda h: (0, h)),
            pl.BlockSpec((1, SEG, POS), lambda h: (h, 0, 0)),
            whole((8, SEG)),
        ),
        scratch_shapes=[
            pltpu.VMEM((SEG, DH), jnp.float32),
            pltpu.VMEM((SEG, DH), jnp.float32),
        ],
        compiler_params=pltpu.CompilerParams(vmem_limit_bytes=48 << 20),
        name="forward",
    )(kept, q, ks, vs, mem, bias, cot, gain)


def backward_kernel(
    stats0_ref, stats1_ref, stats2_ref, stats3_ref,
    q_ref, ks_ref, vs_ref, mem_ref, cot_ref, gain_ref, attn_ref, prob_ref,
    attended_ref, dq_ref, dk_ref, dv_ref, share_ref,
    inv_ref, coef_ref, gain_sum_ref, diag_ref,
):
    head = pl.program_id(0)

    @pl.when(head == 0)
    def _():
        stats = (stats0_ref[...] + stats1_ref[...]) + (stats2_ref[...] + stats3_ref[...])
        inv = lax.rsqrt(stats[0:1] / HD + 1e-06)
        coef = inv * inv * inv * stats[1:2] / HD
        inv_ref[...] = jnp.broadcast_to(inv, (DH, SEG)).T
        coef_ref[...] = jnp.broadcast_to(coef, (DH, SEG)).T
        gain_sum_ref[...] = jnp.zeros((8, DH), jnp.float32)
        diag_ref[...] = jnp.zeros((8, POS), jnp.float32)

    q = q_ref[0]
    attn = attn_ref[...]
    inv = inv_ref[...]
    gain = gain_ref[...]
    upstream = cot_ref[0].astype(jnp.float32)
    normed = attn * inv
    attended_ref[0] = (normed * gain).astype(jnp.bfloat16)
    gain_sum_ref[pl.ds(head, 1), :] = jnp.sum(upstream * normed, axis=0, keepdims=True)
    out_grad = (inv * (upstream * gain) - attn * coef_ref[...]).astype(jnp.bfloat16)
    delta = jnp.sum(out_grad.astype(jnp.float32) * attn, axis=1, keepdims=True)
    w_mem = prob_ref[0, :, :MEM]
    w_seg = prob_ref[0, :, MEM:]
    dp_mem = dot(out_grad, mem_ref[MEM:], NT)
    dp_seg = dot(out_grad, vs_ref[0], NT)
    ds_mem = w_mem.astype(jnp.float32) * (dp_mem - delta)
    ds_seg = w_seg.astype(jnp.float32) * (dp_seg - delta)
    dsb_mem = ds_mem.astype(jnp.bfloat16)
    dsb_seg = ds_seg.astype(jnp.bfloat16)
    dq_ref[0] = (
        (dot(dsb_mem, mem_ref[:MEM], NN) + dot(dsb_seg, ks_ref[0], NN)) * SCALE
    ).astype(jnp.bfloat16)
    dk_ref[0] = (dot(dsb_seg, q, TN) * SCALE).astype(jnp.bfloat16)
    dv_ref[0] = dot(w_seg, out_grad, TN).astype(jnp.bfloat16)
    diag_ref[pl.ds(head, 1), :] = diagonal_row(jnp.concatenate([ds_mem, ds_seg], axis=1))

    @pl.when(head == HEADS - 1)
    def _():
        bias = stagger(by_distance(diag_ref[...]), 8)
        bias = jnp.concatenate([bias, bias[:, :128]], axis=1)
        lane = lax.broadcasted_iota(jnp.int32, (8, DH), 1)
        row = lax.broadcasted_iota(jnp.int32, (8, DH), 0)
        own = (lane >= 8 * row) & (lane < 8 * row + 8) & (row < HEADS)
        gains = gain_sum_ref[...]
        for dest in range(DP):
            start, shift = divmod(8 * dest, 128)
            here = bias[:, 128 * start : 128 * start + 128]
            after = bias[:, 128 * start + 128 : 128 * start + 256]
            part = jnp.where(lane < 128 - shift, roll(here, -shift), roll(after, -shift))
            part = jnp.sum(jnp.where(own, part, 0.0), axis=0, keepdims=True)
            share_ref[dest] = jnp.where(row == HEADS, part, gains)


def backward(stats, q, ks, vs, mem, cot, gain, attn, prob):
    big = jax.ShapeDtypeStruct((1, SEG, COLS), jnp.bfloat16)
    return pl.pallas_call(
        backward_kernel,
        grid=(HEADS,),
        out_shape=(big, big, big, big, jax.ShapeDtypeStruct((DP, 8, DH), jnp.float32)),
        in_specs=[
            whole((8, SEG)),
            whole((8, SEG)),
            whole((8, SEG)),
            whole((8, SEG)),
            column_spec(),
            column_spec(),
            column_spec(),
            pl.BlockSpec((2 * MEM, DH), lambda h: (0, h)),
            column_spec(),
            pl.BlockSpec((1, DH), lambda h: (0, h)),
            pl.BlockSpec((SEG, DH), lambda h: (0, h)),
            pl.BlockSpec((1, SEG, POS), lambda h: (h, 0, 0)),
        ],
        out_specs=(
            column_spec(),
            column_spec(),
            column_spec(),
            column_spec(),
            whole((DP, 8, DH)),
        ),
        scratch_shapes=[
            pltpu.VMEM((SEG, DH), jnp.float32),
            pltpu.VMEM((SEG, DH), jnp.float32),
            pltpu.VMEM((8, DH), jnp.float32),
            pltpu.VMEM((8, POS), jnp.float32),
        ],
        compiler_params=pltpu.CompilerParams(vmem_limit_bytes=48 << 20),
        name="backward",
    )(*stats, q, ks, vs, mem, cot, gain, attn, prob)


def collect_kernel(share_ref, bias_ref, gain_ref):
    total = jnp.sum(share_ref[...], axis=0)
    gain_ref[...] = total[:HEADS]
    bias = stagger(jnp.broadcast_to(total[HEADS : HEADS + 1], (8, DH)), -8)
    bias_ref[...] = bias[:HEADS, :8]


def collect(shares):
    return pl.pallas_call(
        collect_kernel,
        out_shape=(
            jax.ShapeDtypeStruct((HEADS, 8), jnp.float32),
            jax.ShapeDtypeStruct((HEADS, DH), jnp.float32),
        ),
        name="collect",
    )(shares)


def exchange(x):
    return lax.all_to_all(x, "dp", split_axis=0, concat_axis=0, tiled=True)


def body(
    seg_queries, seg_keys, seg_values, memory_keys, memory_values,
    new_owner, kept_blocks, rel_bias, norm_gain, cotangent,
):
    own_index = lax.axis_index("dp")
    kept = jnp.sum(jnp.where(new_owner == own_index, kept_blocks, 0)).reshape(1)
    gain = norm_gain.reshape(1, COLS)
    pieces = jnp.concatenate([memory_keys[0], memory_values[0]], axis=0)
    spread = exchange(pieces.reshape(DP, PIECE, COLS))
    mem = exchange(reorder(new_owner, spread)).reshape(2 * MEM, COLS)
    attn, prob, stats = forward(
        kept, seg_queries, seg_keys, seg_values, mem, rel_bias, cotangent, gain
    )
    others = [
        lax.ppermute(stats, "mp", [(i, (i + step) % 4) for i in range(4)]) for step in (1, 2, 3)
    ]
    attended, query_grad, key_grad, value_grad, shares = backward(
        [stats] + others, seg_queries, seg_keys, seg_values, mem, cotangent, gain, attn, prob
    )
    bias_grad, gain_grad = collect(exchange(shares))
    return attended, query_grad, key_grad, value_grad, bias_grad, gain_grad.reshape(COLS)


def solution(mesh):
    row = P("dp", None, "mp")
    return jax.shard_map(
        body,
        mesh=mesh,
        in_specs=(row, row, row, row, row, P(), P(), P("mp", None), P("mp"), row),
        out_specs=(row, row, row, row, P("mp", "dp"), P("mp")),
        check_vma=False,
    )
```

profile of v0, /device:TPU:1, one launch (start us, length us, event | category | flops | bytes accessed | tf_op | source)
XLA Modules:
  0.0 111.5 jit_solution(7641332249365901095)
XLA Ops:
  0.6 1.2 %maximum_bitcast_fusion = bf16[64,8,768]{2,1,0:T(8,128)(2,1)S(1)} fusion(bf16[256,768]{1,0:T(8,128)(2,1)} %bitcast.9, bf16[256,768]{1,0:T(8,128)(2,1)} %bitcast.10), kind=kLoop, calls=%fused_computation | loop fusion | flops 1572864 | bytes 1572864 | tf_op jit(solution)/shard_map/reshape | solution.py:305
  1.8 36.0 %all_to_all.15.in_ref = bf16[64,8,768]{2,1,0:T(8,128)(2,1)} all-to-all(bf16[64,8,768]{2,1,0:T(8,128)(2,1)S(1)} %maximum_bitcast_fusion), channel_id=1, replica_groups=mesh['dp'=64,'mp'=4] {'dp'}, dimensions={0} | all-to-all | bytes 1572864 | tf_op jit(solution)/shard_map/all_to_all | solution.py:294
  37.8 0.0 copy-start.5
  37.8 0.0 copy-start.6
  37.8 0.0 copy-start.7
  37.9 0.0 copy-start
  37.9 0.0 copy-start.1
  37.9 0.0 copy-start.2
  37.9 0.0 copy-start.3
  37.9 0.0 copy-start.4
  37.9 2.2 %reorder.1 = bf16[64,8,768]{2,1,0:T(8,128)(2,1)} custom-call(s32[64]{0:T(128)} %owner_ref.1, bf16[64,8,768]{2,1,0:T(8,128)(2,1)} %all_to_all.15.in_ref), custom_call_target="tpu_custom_call" | custom-call | tf_op jit(solution)/shard_map/reorder/pallas_call | solution.py:77
  40.2 6.2 %all-to-all-start.1 = ((bf16[64,8,768]{2,1,0:T(8,128)(2,1)}), bf16[64,8,768]{2,1,0:T(8,128)(2,1)S(1)}, u32[]{:S(2)}, u32[]{:S(2)}) async-start(bf16[64,8,768]{2,1,0:T(8,128)(2,1)} %reorder.1), calls=%async_computation.1 | async-start | bytes 1572864 | tf_op jit(solution)/shard_map/all_to_all | solution.py:294
  46.4 0.0 copy-done.5
  46.4 0.0 copy-done.6
  46.4 0.0 copy-done.7
  46.4 0.6 fusion
  47.0 22.3 %all-to-all-done.1 = bf16[64,8,768]{2,1,0:T(8,128)(2,1)S(1)} async-done(((bf16[64,8,768]{2,1,0:T(8,128)(2,1)}), bf16[64,8,768]{2,1,0:T(8,128)(2,1)S(1)}, u32[]{:S(2)}, u32[]{:S(2)}) %all-to-all-start.1) | async-done | bytes 786464 | tf_op jit(solution)/shard_map/all_to_all | solution.py:294
  69.3 0.0 copy-done
  69.3 0.0 copy-done.1
  69.3 0.0 copy-done.2
  69.3 0.0 copy-done.3
  69.4 0.0 copy-done.4
  69.4 6.6 %forward.1 = (f32[256,768]{1,0:T(8,128)S(1)}, bf16[6,256,512]{2,1,0:T(8,128)(2,1)S(1)}, f32[8,256]{1,0:T(8,128)S(1)}) custom-call(s32[1]{0:T(128)} %bitcast.kept_ref, bf16[1,256,768]{2,1,0:T(8,128)(2,1)S(1)} %copy-done, bf16[1,256,768]{2,1,0:T(8,128)(2,1)S(1)} %copy-done.1, bf16[1,256,768]{2,1,0:T(8,128)(2,1)S(1)} %copy-done.2, ...), custom_call_target="tpu_custom_call" | custom-call | tf_op jit(solution)/shard_map/forward/pallas_call | solution.py:145
  76.0 2.6 %collective-permute-start.2 = (f32[8,256]{1,0:T(8,128)S(1)}, f32[8,256]{1,0:T(8,128)S(1)}, u32[]{:S(2)}, u32[]{:S(2)}) collective-permute-start(f32[8,256]{1,0:T(8,128)S(1)} %get-tuple-element.16.stats0_ref), channel_id=1, source_target_pairs={{0,3},{1,0},{2,1},{3,2},{4,7},{5,4},{6,5},{7,6},{8,11},{9,8},{10,9... | collective-permute-start | bytes 24584 | tf_op jit(solution)/shard_map/ppermute | solution.py:311
  78.6 0.5 collective-permute-start.1
  79.1 0.6 collective-permute-start
  79.7 0.0 collective-permute-done.2.stats3_ref
  79.7 2.9 %collective-permute-done.1.stats2_ref = f32[8,256]{1,0:T(8,128)S(1)} collective-permute-done((f32[8,256]{1,0:T(8,128)S(1)}, f32[8,256]{1,0:T(8,128)S(1)}, u32[]{:S(2)}, u32[]{:S(2)}) %collective-permute-start.1) | collective-permute-done | bytes 8224 | tf_op jit(solution)/shard_map/ppermute | solution.py:311
  82.6 0.2 collective-permute-done.stats1_ref
  82.8 7.1 %backward.1 = (bf16[1,256,768]{2,1,0:T(8,128)(2,1)}, bf16[1,256,768]{2,1,0:T(8,128)(2,1)}, bf16[1,256,768]{2,1,0:T(8,128)(2,1)}, bf16[1,256,768]{2,1,0:T(8,128)(2,1)}, f32[64,8,128]{2,1,0:T(8,128)S(1)}) custom-call(f32[8,256]{1,0:T(8,128)S(1)} %get-tuple-element.16.stats0_ref, f32[8,256]{1,0:T(8,128)S(1)} %collective-permute-done.stats1_ref, ...), custom_call_target="tpu_custom_call" | custom-call | tf_op jit(solution)/shard_map/backward/pallas_call | solution.py:239
  89.9 19.8 %all_to_all.16.share_ref = f32[64,8,128]{2,1,0:T(8,128)} all-to-all(f32[64,8,128]{2,1,0:T(8,128)S(1)} %get-tuple-element.23), channel_id=1, replica_groups=mesh['dp'=64,'mp'=4] {'dp'}, dimensions={0} | all-to-all | bytes 524288 | tf_op jit(solution)/shard_map/all_to_all | solution.py:294
  109.7 1.8 %collect.1 = (f32[6,8]{1,0:T(8,128)}, f32[6,128]{1,0:T(8,128)}) custom-call(f32[64,8,128]{2,1,0:T(8,128)} %all_to_all.16.share_ref), custom_call_target="tpu_custom_call" | custom-call | tf_op jit(solution)/shard_map/collect/pallas_call | solution.py:283
  (1 shorter events, 0.0 us)
Async XLA Ops:
  37.8 8.5 %copy-start.5 = (f32[768]{0:T(1024)S(1)}, f32[768]{0:T(1024)}, u32[]{:S(2)}) copy-start(f32[768]{0:T(1024)} %param.18) | copy-start | bytes 9220
  37.8 8.5 %copy-start.6 = (s32[64]{0:T(128)S(1)}, s32[64]{0:T(128)}, u32[]{:S(2)}) copy-start(s32[64]{0:T(128)} %owner_ref.1) | copy-start | bytes 772
  37.8 8.5 %copy-start.7 = (s32[64]{0:T(128)S(1)}, s32[64]{0:T(128)}, u32[]{:S(2)}) copy-start(s32[64]{0:T(128)} %param.16) | copy-start | bytes 772
  37.9 31.5 %copy-start = (bf16[1,256,768]{2,1,0:T(8,128)(2,1)S(1)}, bf16[1,256,768]{2,1,0:T(8,128)(2,1)}, u32[]{:S(2)}) copy-start(bf16[1,256,768]{2,1,0:T(8,128)(2,1)} %q_ref.3) | copy-start | bytes 1179652
  37.9 31.5 %copy-start.1 = (bf16[1,256,768]{2,1,0:T(8,128)(2,1)S(1)}, bf16[1,256,768]{2,1,0:T(8,128)(2,1)}, u32[]{:S(2)}) copy-start(bf16[1,256,768]{2,1,0:T(8,128)(2,1)} %ks_ref.3) | copy-start | bytes 1179652
  37.9 31.5 %copy-start.2 = (bf16[1,256,768]{2,1,0:T(8,128)(2,1)S(1)}, bf16[1,256,768]{2,1,0:T(8,128)(2,1)}, u32[]{:S(2)}) copy-start(bf16[1,256,768]{2,1,0:T(8,128)(2,1)} %vs_ref.3) | copy-start | bytes 1179652
  37.9 31.5 %copy-start.3 = (bf16[1,256,768]{2,1,0:T(8,128)(2,1)S(1)}, bf16[1,256,768]{2,1,0:T(8,128)(2,1)}, u32[]{:S(2)}) copy-start(bf16[1,256,768]{2,1,0:T(8,128)(2,1)} %cot_ref.3) | copy-start | bytes 1179652
  37.9 31.5 %copy-start.4 = (f32[6,512]{1,0:T(8,128)S(1)}, f32[6,512]{1,0:T(8,128)}, u32[]{:S(2)}) copy-start(f32[6,512]{1,0:T(8,128)} %bias_ref.1) | copy-start | bytes 36868
  40.2 29.2 %all-to-all-start.1 = ((bf16[64,8,768]{2,1,0:T(8,128)(2,1)}), bf16[64,8,768]{2,1,0:T(8,128)(2,1)S(1)}, u32[]{:S(2)}, u32[]{:S(2)}) async-start(bf16[64,8,768]{2,1,0:T(8,128)(2,1)} %reorder.1), calls=%async_computation.1 | async-start | bytes 1572864 | tf_op jit(solution)/shard_map/all_to_all | solution.py:294
  76.0 3.7 %collective-permute-start.2 = (f32[8,256]{1,0:T(8,128)S(1)}, f32[8,256]{1,0:T(8,128)S(1)}, u32[]{:S(2)}, u32[]{:S(2)}) collective-permute-start(f32[8,256]{1,0:T(8,128)S(1)} %get-tuple-element.16.stats0_ref), channel_id=1, source_target_pairs={{0,3},{1,0},{2,1},{3,2},{4,7},{5,4},{6,5},{7,6},{8,11},{9,8},{10,9... | collective-permute-start | bytes 24584 | tf_op jit(solution)/shard_map/ppermute | solution.py:311
  78.6 4.0 %collective-permute-start.1 = (f32[8,256]{1,0:T(8,128)S(1)}, f32[8,256]{1,0:T(8,128)S(1)}, u32[]{:S(2)}, u32[]{:S(2)}) collective-permute-start(f32[8,256]{1,0:T(8,128)S(1)} %get-tuple-element.16.stats0_ref), channel_id=1, source_target_pairs={{0,2},{1,3},{2,0},{3,1},{4,6},{5,7},{6,4},{7,5},{8,10},{9,11},{10,... | collective-permute-start | bytes 24584 | tf_op jit(solution)/shard_map/ppermute | solution.py:311
  79.1 3.7 %collective-permute-start = (f32[8,256]{1,0:T(8,128)S(1)}, f32[8,256]{1,0:T(8,128)S(1)}, u32[]{:S(2)}, u32[]{:S(2)}) collective-permute-start(f32[8,256]{1,0:T(8,128)S(1)} %get-tuple-element.16.stats0_ref), channel_id=1, source_target_pairs={{0,1},{1,2},{2,3},{3,0},{4,5},{5,6},{6,7},{7,4},{8,9},{9,10},{10,1... | collective-permute-start | bytes 24584 | tf_op jit(solution)/shard_map/ppermute | solution.py:311
where the time goes:
time: 112 us
  blocking collectives  55.8 us (50%)
  waiting for transfers between devices  25.4 us (23%)
  Pallas kernels  17.8 us (16%)
  starting transfers between devices  9.88 us (9%)
  other arithmetic  1.8 us (2%)
    all_to_all x2, blocking collectives, exchange(): return lax.all_to_all(x, 'dp', split_axis=0, concat_axis=0, tiled=True)  55.8 us
    all_to_all x1, waiting for transfers between devices, exchange(): return lax.all_to_all(x, 'dp', split_axis=0, concat_axis=0, tiled=True)  22.3 us
    pallas_call x1, Pallas kernels, backward(): pl.pallas_call(backward_kernel, grid=(HEADS,), out_shape=(big, big, big,...  7.11 us
    pallas_call x1, Pallas kernels, forward(): pl.pallas_call(forward_kernel, grid=(HEADS,), out_shape=(jax.ShapeDtypeSt...  6.62 us
    all_to_all x1, starting transfers between devices, exchange(): return lax.all_to_all(x, 'dp', split_axis=0, concat_axis=0, tiled=True)  6.19 us
    ppermute x3, starting transfers between devices, body(): lax.ppermute(stats, 'mp', [(i, (i + step) % 4) for i in range(4)])  3.68 us
    ppermute x3, waiting for transfers between devices, body(): lax.ppermute(stats, 'mp', [(i, (i + step) % 4) for i in range(4)])  3.11 us
    pallas_call x1, Pallas kernels, reorder(): pl.pallas_call(reorder_kernel, out_shape=jax.ShapeDtypeStruct(pieces.shap...  2.25 us
  transfers between devices with their start and end apart: 4, of which 3 were waited for; matrix products, arithmetic and copies ran while one was open for 1% of the time, Pallas kernels for 0%

commit v1 on v0

v1 whole, which is shorter than its diff:
```python
import math

import jax
import jax.numpy as jnp
from jax import lax
from jax.experimental import pallas as pl
from jax.experimental.pallas import tpu as pltpu
from jax.sharding import PartitionSpec as P

DH = 128
BLOCK = 128
HD = 3072
SEG = 256
MEM = 256
POS = 512
HEADS = 6
COLS = HEADS * DH
DP = 64
PIECE = (2 * MEM) // DP
LOG2E = math.log2(math.e)
SCALE = DH ** (-0.5)
FACTOR = SCALE * LOG2E
GROUP = 2
STEPS = HEADS // GROUP
NT = (((1,), (1,)), ((), ()))
NN = (((1,), (0,)), ((), ()))
TN = (((0,), (0,)), ((), ()))


def dot(a, b, dims):
    return lax.dot_general(a, b, dims, preferred_element_type=jnp.float32)


def roll(x, shift):
    shift = shift % x.shape[1]
    return x if shift == 0 else pltpu.roll(x, shift, axis=1)


def reverse_lanes(x):
    rows, width = x.shape
    index = 127 - lax.broadcasted_iota(jnp.int32, (rows, 128), 1)
    parts = [
        jnp.take_along_axis(x[:, start : start + 128], index, axis=1)
        for start in range(width - 128, -1, -128)
    ]
    return jnp.concatenate(parts, axis=1)


def by_distance(x):
    return roll(reverse_lanes(x), -255)


def stagger(x, unit):
    row = lax.broadcasted_iota(jnp.int32, x.shape, 0)
    for bit in (1, 2, 4):
        x = jnp.where((row & bit) != 0, roll(x, bit * unit), x)
    return x


def bias_rows(table_row):
    base = stagger(jnp.broadcast_to(by_distance(jnp.broadcast_to(table_row, (8, POS))), (8, POS)), 1)
    return jnp.concatenate([roll(base, 8 * group) for group in range(SEG // 8)], axis=0)


def diagonal_row(score_grad):
    level = [score_grad[8 * g : 8 * g + 8] for g in range(SEG // 8)]
    shift = 8
    while len(level) > 1:
        level = [level[k] + roll(level[k + 1], -shift) for k in range(0, len(level), 2)]
        shift *= 2
    return jnp.sum(stagger(level[0], -1), axis=0, keepdims=True)


def reorder_kernel(owner_ref, in_ref, out_ref):
    for slot in range(DP):
        out_ref[owner_ref[slot]] = in_ref[slot]


def reorder(new_owner, pieces):
    return pl.pallas_call(
        reorder_kernel,
        out_shape=jax.ShapeDtypeStruct(pieces.shape, pieces.dtype),
        in_specs=[
            pl.BlockSpec(memory_space=pltpu.SMEM),
            pl.BlockSpec(memory_space=pltpu.VMEM),
        ],
        out_specs=pl.BlockSpec(memory_space=pltpu.VMEM),
        name="reorder",
    )(new_owner, pieces)


def segment_kernel(
    kept_ref, q_ref, ks_ref, vs_ref, bias_ref,
    prob_ref, out_ref, top_ref, total_ref, mem_bias_ref,
):
    col = lax.broadcasted_iota(jnp.int32, (SEG, MEM), 1)
    row = lax.broadcasted_iota(jnp.int32, (SEG, MEM), 0)
    ones = jnp.ones((SEG, DH), jnp.bfloat16)
    for g in range(GROUP):
        head = pl.program_id(0) * GROUP + g
        cols = slice(DH * g, DH * g + DH)
        bias = bias_rows(bias_ref[pl.ds(head, 1), :] * LOG2E)
        mem_bias_ref[g] = jnp.where(col >= MEM - BLOCK * kept_ref[0], bias[:, :MEM], -1e30)
        scores = dot(q_ref[0, :, cols], ks_ref[0, :, cols], NT) * FACTOR + bias[:, MEM:]
        scores = jnp.where(col <= row, scores, -1e30)
        top = jnp.max(scores, axis=1, keepdims=True)
        prob = jnp.exp2(scores - top).astype(jnp.bfloat16)
        prob_ref[g] = prob
        both = dot(prob, jnp.concatenate([vs_ref[0, :, cols], ones], axis=1), NN)
        out_ref[:, cols] = both[:, :DH]
        total_ref[:, cols] = both[:, DH:]
        top_ref[:, cols] = jnp.broadcast_to(top, (SEG, DH))


def forward_kernel(
    q_ref, mem_ref, mem_bias_ref, cot_ref, gain_ref, seg_out_ref, seg_top_ref, seg_total_ref,
    out_ref, prob_ref, factor_mem_ref, factor_seg_ref, stats_ref, square_ref, cross_ref,
):
    step = pl.program_id(0)
    ones = jnp.ones((MEM, DH), jnp.bfloat16)
    square = cross = None
    for g in range(GROUP):
        cols = slice(DH * g, DH * g + DH)
        scores = dot(q_ref[0, :, cols], mem_ref[:MEM, cols], NT) * FACTOR + mem_bias_ref[g]
        seg_top = seg_top_ref[:, cols]
        top = jnp.maximum(jnp.max(scores, axis=1, keepdims=True), seg_top)
        prob = jnp.exp2(scores - jnp.concatenate([top, top], axis=1)).astype(jnp.bfloat16)
        prob_ref[g] = prob
        both = dot(prob, jnp.concatenate([mem_ref[MEM:, cols], ones], axis=1), NN)
        shrink = jnp.exp2(seg_top - top)
        inverse = 1.0 / (both[:, DH:] + seg_total_ref[:, cols] * shrink)
        factor_seg = shrink * inverse
        out = both[:, :DH] * inverse + seg_out_ref[:, cols] * factor_seg
        factor_mem_ref[:, cols] = inverse
        factor_seg_ref[:, cols] = factor_seg
        out_ref[:, cols] = out
        part = cot_ref[0, :, cols].astype(jnp.float32) * gain_ref[:, cols] * out
        square = out * out if g == 0 else square + out * out
        cross = part if g == 0 else cross + part

    @pl.when(step == 0)
    def _():
        square_ref[...] = square
        cross_ref[...] = cross

    @pl.when(step > 0)
    def _():
        square_ref[...] += square
        cross_ref[...] += cross

    @pl.when(step == STEPS - 1)
    def _():
        stats_ref[...] = jnp.zeros((8, SEG), jnp.float32)
        stats_ref[0:1, :] = jnp.sum(square_ref[...].T, axis=0, keepdims=True)
        stats_ref[1:2, :] = jnp.sum(cross_ref[...].T, axis=0, keepdims=True)


def score_grad_kernel(
    stats0_ref, stats1_ref, stats2_ref, stats3_ref,
    vs_ref, mem_ref, cot_ref, gain_ref, attn_ref, prob_mem_ref, prob_seg_ref,
    factor_mem_ref, factor_seg_ref,
    ds_mem_ref, ds_seg_ref, og_seg_ref, attended_ref, share_ref,
    inv_ref, coef_ref, gain_sum_ref, diag_ref,
):
    step = pl.program_id(0)

    @pl.when(step == 0)
    def _():
        stats = (stats0_ref[...] + stats1_ref[...]) + (stats2_ref[...] + stats3_ref[...])
        inv = lax.rsqrt(stats[0:1] / HD + 1e-06)
        coef = inv * inv * inv * stats[1:2] / HD
        inv_ref[...] = jnp.broadcast_to(inv, (DH, SEG)).T
        coef_ref[...] = jnp.broadcast_to(coef, (DH, SEG)).T
        gain_sum_ref[...] = jnp.zeros((8, DH), jnp.float32)
        diag_ref[...] = jnp.zeros((8, POS), jnp.float32)

    inv = inv_ref[...]
    coef = coef_ref[...]
    for g in range(GROUP):
        head = step * GROUP + g
        cols = slice(DH * g, DH * g + DH)
        attn = attn_ref[:, cols]
        gain = gain_ref[:, cols]
        upstream = cot_ref[0, :, cols].astype(jnp.float32)
        normed = attn * inv
        attended_ref[0, :, cols] = (normed * gain).astype(jnp.bfloat16)
        gain_sum_ref[pl.ds(head, 1), :] = jnp.sum(upstream * normed, axis=0, keepdims=True)
        out_grad = inv * (upstream * gain) - attn * coef
        delta = jnp.sum(out_grad * attn, axis=1, keepdims=True)
        factor_mem = factor_mem_ref[:, cols]
        factor_seg = factor_seg_ref[:, cols]
        og_mem = (out_grad * factor_mem).astype(jnp.bfloat16)
        og_seg = (out_grad * factor_seg).astype(jnp.bfloat16)
        og_seg_ref[:, cols] = og_seg
        less_mem = delta * factor_mem
        less_seg = delta * factor_seg
        dp_mem = dot(og_mem, mem_ref[:, cols], NT) - jnp.concatenate([less_mem, less_mem], axis=1)
        dp_seg = dot(og_seg, vs_ref[0, :, cols], NT) - jnp.concatenate([less_seg, less_seg], axis=1)
        ds_mem = prob_mem_ref[g].astype(jnp.float32) * dp_mem
        ds_seg = prob_seg_ref[g].astype(jnp.float32) * dp_seg
        ds_mem_ref[g] = ds_mem.astype(jnp.bfloat16)
        ds_seg_ref[g] = ds_seg.astype(jnp.bfloat16)
        diag_ref[pl.ds(head, 1), :] = diagonal_row(jnp.concatenate([ds_mem, ds_seg], axis=1))

    @pl.when(step == STEPS - 1)
    def _():
        bias = stagger(by_distance(diag_ref[...]), 8)
        bias = jnp.concatenate([bias, bias[:, :128]], axis=1)
        lane = lax.broadcasted_iota(jnp.int32, (8, DH), 1)
        row = lax.broadcasted_iota(jnp.int32, (8, DH), 0)
        own = (lane >= 8 * row) & (lane < 8 * row + 8) & (row < HEADS)
        gains = gain_sum_ref[...]
        for dest in range(DP):
            start, shift = divmod(8 * dest, 128)
            here = bias[:, 128 * start : 128 * start + 128]
            after = bias[:, 128 * start + 128 : 128 * start + 256]
            part = jnp.where(lane < 128 - shift, roll(here, -shift), roll(after, -shift))
            part = jnp.sum(jnp.where(own, part, 0.0), axis=0, keepdims=True)
            share_ref[dest] = jnp.where(row == HEADS, part, gains).astype(share_ref.dtype)


def input_grad_kernel(
    q_ref, ks_ref, mem_ref, ds_mem_ref, ds_seg_ref, prob_seg_ref, og_seg_ref,
    dq_ref, dk_ref, dv_ref,
):
    for g in range(GROUP):
        cols = slice(DH * g, DH * g + DH)
        ds_seg = ds_seg_ref[g]
        dq = dot(ds_mem_ref[g], mem_ref[:, cols], NN) + dot(ds_seg, ks_ref[0, :, cols], NN)
        dq_ref[0, :, cols] = (dq * SCALE).astype(jnp.bfloat16)
        dk_ref[0, :, cols] = (dot(ds_seg, q_ref[0, :, cols], TN) * SCALE).astype(jnp.bfloat16)
        dv_ref[0, :, cols] = dot(prob_seg_ref[g], og_seg_ref[:, cols], TN).astype(jnp.bfloat16)


def token_spec():
    return pl.BlockSpec((1, SEG, DH * GROUP), lambda h: (0, 0, h))


def column_spec():
    return pl.BlockSpec((SEG, DH * GROUP), lambda h: (0, h))


def square_spec():
    return pl.BlockSpec((GROUP, SEG, SEG), lambda h: (h, 0, 0))


def gain_spec():
    return pl.BlockSpec((1, DH * GROUP), lambda h: (0, h))


def keys_spec():
    return pl.BlockSpec((MEM, DH * GROUP), lambda h: (0, h))


def values_spec():
    return pl.BlockSpec((MEM, DH * GROUP), lambda h: (1, h))


def both_spec():
    return pl.BlockSpec((2 * MEM, DH * GROUP), lambda h: (0, h))


def whole(*shape):
    return pl.BlockSpec(shape, lambda h: (0,) * len(shape))


TOKENS = jax.ShapeDtypeStruct((1, SEG, COLS), jnp.bfloat16)
COLUMNS = jax.ShapeDtypeStruct((SEG, COLS), jnp.float32)
COLUMNS_B = jax.ShapeDtypeStruct((SEG, COLS), jnp.bfloat16)
SQUARES = jax.ShapeDtypeStruct((HEADS, SEG, SEG), jnp.float32)
SQUARES_B = jax.ShapeDtypeStruct((HEADS, SEG, SEG), jnp.bfloat16)


def call(kernel, in_specs, outs, scratch=()):
    return pl.pallas_call(
        kernel,
        grid=(STEPS,),
        in_specs=in_specs,
        out_shape=tuple(shape for shape, _ in outs),
        out_specs=tuple(spec for _, spec in outs),
        scratch_shapes=[pltpu.VMEM(shape, jnp.float32) for shape in scratch],
        compiler_params=pltpu.CompilerParams(vmem_limit_bytes=48 << 20),
        name=kernel.__name__,
    )


def segment(kept, q, ks, vs, bias):
    return call(
        segment_kernel,
        [pl.BlockSpec(memory_space=pltpu.SMEM)] + [token_spec()] * 3 + [whole(HEADS, POS)],
        [
            (SQUARES_B, square_spec()),
            (COLUMNS, column_spec()),
            (COLUMNS, column_spec()),
            (COLUMNS, column_spec()),
            (SQUARES, square_spec()),
        ],
    )(kept, q, ks, vs, bias)


def forward(q, mem, mem_bias, cot, gain, seg_out, seg_top, seg_total):
    return call(
        forward_kernel,
        [token_spec(), both_spec(), square_spec(), token_spec(), gain_spec()]
        + [column_spec()] * 3,
        [
            (COLUMNS, column_spec()),
            (SQUARES_B, square_spec()),
            (COLUMNS, column_spec()),
            (COLUMNS, column_spec()),
            (jax.ShapeDtypeStruct((8, SEG), jnp.float32), whole(8, SEG)),
        ],
        [(SEG, DH), (SEG, DH)],
    )(q, mem, mem_bias, cot, gain, seg_out, seg_top, seg_total)


def score_grad(stats, vs, mem, cot, gain, attn, prob_mem, prob_seg, factor_mem, factor_seg):
    return call(
        score_grad_kernel,
        [whole(8, SEG)] * 4
        + [token_spec(), values_spec(), token_spec(), gain_spec(), column_spec()]
        + [square_spec()] * 2
        + [column_spec()] * 2,
        [
            (SQUARES_B, square_spec()),
            (SQUARES_B, square_spec()),
            (COLUMNS_B, column_spec()),
            (TOKENS, token_spec()),
            (jax.ShapeDtypeStruct((DP, 8, DH), jnp.bfloat16), whole(DP, 8, DH)),
        ],
        [(SEG, DH), (SEG, DH), (8, DH), (8, POS)],
    )(*stats, vs, mem, cot, gain, attn, prob_mem, prob_seg, factor_mem, factor_seg)


def input_grad(q, ks, mem, ds_mem, ds_seg, prob_seg, og_seg):
    return call(
        input_grad_kernel,
        [token_spec(), token_spec(), keys_spec()] + [square_spec()] * 3 + [column_spec()],
        [(TOKENS, token_spec())] * 3,
    )(q, ks, mem, ds_mem, ds_seg, prob_seg, og_seg)


def collect_kernel(share_ref, bias_ref, gain_ref):
    total = jnp.sum(share_ref[...].astype(jnp.float32), axis=0)
    gain_ref[...] = total[:HEADS]
    bias = stagger(jnp.broadcast_to(total[HEADS : HEADS + 1], (8, DH)), -8)
    bias_ref[...] = bias[:HEADS, :8]


def collect(shares):
    return pl.pallas_call(
        collect_kernel,
        out_shape=(
            jax.ShapeDtypeStruct((HEADS, 8), jnp.float32),
            jax.ShapeDtypeStruct((HEADS, DH), jnp.float32),
        ),
        name="collect",
    )(shares)


def exchange(x):
    return lax.all_to_all(x, "dp", split_axis=0, concat_axis=0, tiled=True)


def body(
    seg_queries, seg_keys, seg_values, memory_keys, memory_values,
    new_owner, kept_blocks, rel_bias, norm_gain, cotangent,
):
    own_index = lax.axis_index("dp")
    kept = jnp.sum(jnp.where(new_owner == own_index, kept_blocks, 0)).reshape(1)
    gain = norm_gain.reshape(1, COLS)
    pieces = jnp.concatenate([memory_keys[0], memory_values[0]], axis=0)
    spread = exchange(pieces.reshape(DP, PIECE, COLS))
    mem = exchange(reorder(new_owner, spread)).reshape(2 * MEM, COLS)
    prob_seg, seg_out, seg_top, seg_total, mem_bias = segment(
        kept, seg_queries, seg_keys, seg_values, rel_bias
    )
    attn, prob_mem, factor_mem, factor_seg, stats = forward(
        seg_queries, mem, mem_bias, cotangent, gain, seg_out, seg_top, seg_total
    )
    others = [
        lax.ppermute(stats, "mp", [(i, (i + step) % 4) for i in range(4)]) for step in (1, 2, 3)
    ]
    ds_mem, ds_seg, og_seg, attended, shares = score_grad(
        [stats] + others, seg_values, mem, cotangent, gain, attn,
        prob_mem, prob_seg, factor_mem, factor_seg,
    )
    query_grad, key_grad, value_grad = input_grad(
        seg_queries, seg_keys, mem, ds_mem, ds_seg, prob_seg, og_seg
    )
    bias_grad, gain_grad = collect(exchange(shares))
    return attended, query_grad, key_grad, value_grad, bias_grad, gain_grad.reshape(COLS)


def solution(mesh):
    row = P("dp", None, "mp")
    return jax.shard_map(
        body,
        mesh=mesh,
        in_specs=(row, row, row, row, row, P(), P(), P("mp", None), P("mp"), row),
        out_specs=(row, row, row, row, P("mp", "dp"), P("mp")),
        check_vma=False,
    )
```

time: 112 us -> 111 us (level)
  blocking collectives: 55.8 us -> 36 us
  local copies, waits for them, and re-layouts: 0.04 us -> 11.6 us
  starting transfers between devices: 9.88 us -> 18 us
  waiting for transfers between devices: 25.4 us -> 23.1 us
  Pallas kernels: 17.8 us -> 19.5 us
    all_to_all x2 -> x1, blocking collectives: 55.8 us -> 36 us  [exchange(): return lax.all_to_all(x, 'dp', split_axis=0, concat_axis=0, tiled=True)]
    unnamed x16 -> x40, local copies, waits for them, and re-layouts: 0.04 us -> 11.6 us
    all_to_all x1 -> x2, starting transfers between devices: 6.19 us -> 14.4 us  [exchange(): return lax.all_to_all(x, 'dp', split_axis=0, concat_axis=0, tiled=True)]
    all_to_all x1 -> x2, waiting for transfers between devices: 22.3 us -> 20 us  [exchange(): return lax.all_to_all(x, 'dp', split_axis=0, concat_axis=0, tiled=True)]
    pallas_call x2 -> x4, Pallas kernels: 13.7 us -> 15.5 us  [the longest x1 5.24 us: score_grad(): call(score_grad_kernel, [whole(8, SEG)] * 4 + [token_spec(), values_spec(...]
  transfers between devices with their start and end apart: 4 -> 5, of which waited for: 3 -> 4; matrix products, arithmetic and copies ran while one was open for 1% -> 1% of each run, Pallas kernels for 0% -> 6%
where the time goes in v1:
time: 111 us
  blocking collectives  36 us (32%)
  waiting for transfers between devices  23.1 us (21%)
  Pallas kernels  19.5 us (18%)
  starting transfers between devices  18 us (16%)
  local copies, waits for them, and re-layouts  11.6 us (10%)
  other arithmetic  1.8 us (2%)
    all_to_all x1, blocking collectives, exchange(): return lax.all_to_all(x, 'dp', split_axis=0, concat_axis=0, tiled=True)  36 us
    all_to_all x2, waiting for transfers between devices, exchange(): return lax.all_to_all(x, 'dp', split_axis=0, concat_axis=0, tiled=True)  20 us
    all_to_all x2, starting transfers between devices, exchange(): return lax.all_to_all(x, 'dp', split_axis=0, concat_axis=0, tiled=True)  14.4 us
    unnamed x40, local copies, waits for them, and re-layouts  11.6 us
    pallas_call x1, Pallas kernels, score_grad(): call(score_grad_kernel, [whole(8, SEG)] * 4 + [token_spec(), values_spec(...  5.24 us
    pallas_call x1, Pallas kernels, segment(): call(segment_kernel, [pl.BlockSpec(memory_space=pltpu.SMEM)] + [token_spe...  4.11 us
    pallas_call x1, Pallas kernels, forward(): call(forward_kernel, [token_spec(), both_spec(), square_spec(), token_spe...  3.79 us
    ppermute x3, starting transfers between devices, body(): lax.ppermute(stats, 'mp', [(i, (i + step) % 4) for i in range(4)])  3.61 us
  transfers between devices with their start and end apart: 5, of which 4 were waited for; matrix products, arithmetic and copies ran while one was open for 1% of the time, Pallas kernels for 6%

profile of v1, /device:TPU:1, one launch (start us, length us, event | category | flops | bytes accessed | tf_op | source)
XLA Modules:
  0.0 110.8 jit_solution(4838912558581576556)
XLA Ops:
  0.6 1.2 %maximum_bitcast_fusion = bf16[64,8,768]{2,1,0:T(8,128)(2,1)S(1)} fusion(bf16[256,768]{1,0:T(8,128)(2,1)} %bitcast.10, bf16[256,768]{1,0:T(8,128)(2,1)} %bitcast.11), kind=kLoop, calls=%fused_computation | loop fusion | flops 1572864 | bytes 1572864 | tf_op jit(solution)/shard_map/reshape | solution.py:373
  1.8 36.0 %all_to_all.15.in_ref = bf16[64,8,768]{2,1,0:T(8,128)(2,1)} all-to-all(bf16[64,8,768]{2,1,0:T(8,128)(2,1)S(1)} %maximum_bitcast_fusion), channel_id=1, replica_groups=mesh['dp'=64,'mp'=4] {'dp'}, dimensions={0} | all-to-all | bytes 1572864 | tf_op jit(solution)/shard_map/all_to_all | solution.py:362
  37.8 0.0 copy-start.17
  37.8 0.0 copy-start.18
  37.8 0.0 copy-start.19
  37.9 0.0 copy-start
  37.9 0.0 copy-start.2
  37.9 0.0 copy-start.3
  37.9 0.0 copy-start.16
  37.9 2.2 %reorder.1 = bf16[64,8,768]{2,1,0:T(8,128)(2,1)} custom-call(s32[64]{0:T(128)} %owner_ref.1, bf16[64,8,768]{2,1,0:T(8,128)(2,1)} %all_to_all.15.in_ref), custom_call_target="tpu_custom_call" | custom-call | tf_op jit(solution)/shard_map/reorder/pallas_call | solution.py:80
  40.1 0.0 copy-start.1
  40.1 6.3 %all-to-all-start.1 = ((bf16[64,8,768]{2,1,0:T(8,128)(2,1)}), bf16[64,8,768]{2,1,0:T(8,128)(2,1)S(1)}, u32[]{:S(2)}, u32[]{:S(2)}) async-start(bf16[64,8,768]{2,1,0:T(8,128)(2,1)} %reorder.1), calls=%async_computation.1 | async-start | bytes 1572864 | tf_op jit(solution)/shard_map/all_to_all | solution.py:362
  46.4 0.0 copy-done.17
  46.5 0.0 copy-done.18
  46.5 0.0 copy-done.19
  46.5 0.6 fusion
  47.1 0.0 copy-done
  47.1 0.0 copy-done.2
  47.1 0.0 copy-done.3
  47.1 0.0 copy-done.16
  47.1 4.1 %segment_kernel.1 = (bf16[6,256,256]{2,1,0:T(8,128)(2,1)S(1)}, f32[256,768]{1,0:T(8,128)S(1)}, f32[256,768]{1,0:T(8,128)S(1)}, f32[256,768]{1,0:T(8,128)S(1)}, f32[6,256,256]{2,1,0:T(8,128)S(1)}) custom-call(s32[1]{0:T(128)} %bitcast.4.kept_ref, bf16[1,256,768]{2,1,0:T(8,128)(2,1)S(1)} %copy-done, bf16[1,256,768]{2,1,0:T(8,128)(2,1)S(1)} %copy-done.3, ...), custom_call_target="tpu_custom_call" | custom-call | tf_op jit(solution)/shard_map/segment_kernel/pallas_call | solution.py:288
  51.3 0.0 copy-start.4
  51.3 1.2 %copy-done.4 = f32[6,256,256]{2,1,0:T(8,128)} copy-done((f32[6,256,256]{2,1,0:T(8,128)}, f32[6,256,256]{2,1,0:T(8,128)S(1)}, u32[]{:S(2)}) %copy-start.4) | copy-done | bytes 1572888
  52.4 0.0 copy-start.11
  52.4 0.9 copy-done.11
  53.3 0.0 copy-start.13
  53.3 0.9 copy-done.13
  54.2 0.0 copy-start.14
  54.2 0.9 copy-done.14
  55.1 14.3 %all-to-all-done.1 = bf16[64,8,768]{2,1,0:T(8,128)(2,1)S(1)} async-done(((bf16[64,8,768]{2,1,0:T(8,128)(2,1)}), bf16[64,8,768]{2,1,0:T(8,128)(2,1)S(1)}, u32[]{:S(2)}, u32[]{:S(2)}) %all-to-all-start.1) | async-done | bytes 786464 | tf_op jit(solution)/shard_map/all_to_all | solution.py:362
  69.4 0.0 copy-done.1
  69.4 0.0 copy-start.12
  69.4 1.1 %copy-done.12 = f32[256,768]{1,0:T(8,128)S(1)} copy-done((f32[256,768]{1,0:T(8,128)S(1)}, f32[256,768]{1,0:T(8,128)}, u32[]{:S(2)}) %copy-start.12) | copy-done | bytes 786456
  70.6 3.8 %forward_kernel.1 = (f32[256,768]{1,0:T(8,128)S(1)}, bf16[6,256,256]{2,1,0:T(8,128)(2,1)S(1)}, f32[256,768]{1,0:T(8,128)S(1)}, f32[256,768]{1,0:T(8,128)S(1)}, f32[8,256]{1,0:T(8,128)S(1)}) custom-call(bf16[1,256,768]{2,1,0:T(8,128)(2,1)S(1)} %copy-done, bf16[512,768]{1,0:T(8,128)(2,1)S(1)} %bitcast.7, f32[6,256,256]{2,1,0:T(8,128)} %copy-done.4, ...), custom_call_target="tpu_custom_call" | custom-call | tf_op jit(solution)/shard_map/forward_kernel/pallas_call | solution.py:302
  74.4 0.0 copy-start.5
  74.4 0.9 copy-done.5
  75.3 0.0 copy-start.6
  75.3 0.9 copy-done.6
  76.2 2.5 %collective-permute-start.2 = (f32[8,256]{1,0:T(8,128)S(1)}, f32[8,256]{1,0:T(8,128)S(1)}, u32[]{:S(2)}, u32[]{:S(2)}) collective-permute-start(f32[8,256]{1,0:T(8,128)S(1)} %get-tuple-element.30.stats0_ref), channel_id=1, source_target_pairs={{0,3},{1,0},{2,1},{3,2},{4,7},{5,4},{6,5},{7,6},{8,11},{9,8},{10,9... | collective-permute-start | bytes 24584 | tf_op jit(solution)/shard_map/ppermute | solution.py:382
  78.7 0.5 collective-permute-start.1
  79.2 0.6 collective-permute-start
  79.8 0.0 collective-permute-done.2.stats3_ref
  79.8 2.9 %collective-permute-done.1.stats2_ref = f32[8,256]{1,0:T(8,128)S(1)} collective-permute-done((f32[8,256]{1,0:T(8,128)S(1)}, f32[8,256]{1,0:T(8,128)S(1)}, u32[]{:S(2)}, u32[]{:S(2)}) %collective-permute-start.1) | collective-permute-done | bytes 8224 | tf_op jit(solution)/shard_map/ppermute | solution.py:382
  82.7 0.2 collective-permute-done.stats1_ref
  82.9 5.2 %score_grad_kernel.1 = (bf16[6,256,256]{2,1,0:T(8,128)(2,1)S(1)}, bf16[6,256,256]{2,1,0:T(8,128)(2,1)S(1)}, bf16[256,768]{1,0:T(8,128)(2,1)S(1)}, bf16[1,256,768]{2,1,0:T(8,128)(2,1)}, bf16[64,8,128]{2,1,0:T(8,128)(2,1)S(1)}) custom-call(f32[8,256]{1,0:T(8,128)S(1)} %get-tuple-element.30.stats0_ref, f32[8,256]{1,0:T(8,128)S(1)} %collective-permute-done.stats1_ref, ...), custom_call_target="tpu_custom_call" | custom-call | tf_op jit(solution)/shard_map/score_grad_kernel/pallas_call | solution.py:318
  88.1 0.0 copy-start.7
  88.1 0.9 copy-done.7
  89.0 0.0 copy-start.9
  89.0 0.9 copy-done.9
  90.0 0.0 copy-start.15
  90.0 0.6 copy-done.15
  90.6 8.1 %all-to-all-start.2 = ((bf16[64,8,128]{2,1,0:T(8,128)(2,1)}), bf16[64,8,128]{2,1,0:T(8,128)(2,1)}, u32[]{:S(2)}, u32[]{:S(2)}) async-start(bf16[64,8,128]{2,1,0:T(8,128)(2,1)} %copy-done.15), calls=%async_computation.2 | async-start | bytes 262144 | tf_op jit(solution)/shard_map/all_to_all | solution.py:362
  98.7 0.0 copy-start.8
  98.7 1.1 %copy-done.8 = bf16[6,256,256]{2,1,0:T(8,128)(2,1)S(1)} copy-done((bf16[6,256,256]{2,1,0:T(8,128)(2,1)S(1)}, bf16[6,256,256]{2,1,0:T(8,128)(2,1)}, u32[]{:S(2)}) %copy-start.8) | copy-done | bytes 786456
  99.9 0.0 copy-start.10
  99.9 1.1 %copy-done.10 = bf16[6,256,256]{2,1,0:T(8,128)(2,1)S(1)} copy-done((bf16[6,256,256]{2,1,0:T(8,128)(2,1)S(1)}, bf16[6,256,256]{2,1,0:T(8,128)(2,1)}, u32[]{:S(2)}) %copy-start.10) | copy-done | bytes 786456
  101.0 2.4 %input_grad_kernel.1 = (bf16[1,256,768]{2,1,0:T(8,128)(2,1)}, bf16[1,256,768]{2,1,0:T(8,128)(2,1)}, bf16[1,256,768]{2,1,0:T(8,128)(2,1)}) custom-call(bf16[1,256,768]{2,1,0:T(8,128)(2,1)S(1)} %copy-done, bf16[1,256,768]{2,1,0:T(8,128)(2,1)S(1)} %copy-done.3, bf16[512,768]{1,0:T(8,128)(2,1)S(1)} %bitcast.9, bf16[6,256,256]{2,1,0:T(8,128)(2,1)S(1)} %copy-done.8, ...), custom_call_target="tpu_custom_call" | custom-call | tf_op jit(solution)/shard_map/input_grad_kernel/pallas_call | solution.py:336
  103.4 5.6 %all-to-all-done.2.share_ref = bf16[64,8,128]{2,1,0:T(8,128)(2,1)} async-done(((bf16[64,8,128]{2,1,0:T(8,128)(2,1)}), bf16[64,8,128]{2,1,0:T(8,128)(2,1)}, u32[]{:S(2)}, u32[]{:S(2)}) %all-to-all-start.2) | async-done | bytes 131104 | tf_op jit(solution)/shard_map/all_to_all | solution.py:362
  109.0 1.8 %collect.1 = (f32[6,8]{1,0:T(8,128)}, f32[6,128]{1,0:T(8,128)}) custom-call(bf16[64,8,128]{2,1,0:T(8,128)(2,1)} %all-to-all-done.2.share_ref), custom_call_target="tpu_custom_call" | custom-call | tf_op jit(solution)/shard_map/collect/pallas_call | solution.py:351
  (1 shorter events, 0.0 us)
Async XLA Ops:
  37.8 8.6 %copy-start.17 = (f32[768]{0:T(1024)S(1)}, f32[768]{0:T(1024)}, u32[]{:S(2)}) copy-start(f32[768]{0:T(1024)} %param.18) | copy-start | bytes 9220
  37.8 8.6 %copy-start.18 = (s32[64]{0:T(128)S(1)}, s32[64]{0:T(128)}, u32[]{:S(2)}) copy-start(s32[64]{0:T(128)} %owner_ref.1) | copy-start | bytes 772
  37.8 8.6 %copy-start.19 = (s32[64]{0:T(128)S(1)}, s32[64]{0:T(128)}, u32[]{:S(2)}) copy-start(s32[64]{0:T(128)} %param.16) | copy-start | bytes 772
  37.9 9.3 %copy-start = (bf16[1,256,768]{2,1,0:T(8,128)(2,1)S(1)}, bf16[1,256,768]{2,1,0:T(8,128)(2,1)}, u32[]{:S(2)}) copy-start(bf16[1,256,768]{2,1,0:T(8,128)(2,1)} %q_ref.5) | copy-start | bytes 1179652
  37.9 9.3 %copy-start.2 = (bf16[1,256,768]{2,1,0:T(8,128)(2,1)S(1)}, bf16[1,256,768]{2,1,0:T(8,128)(2,1)}, u32[]{:S(2)}) copy-start(bf16[1,256,768]{2,1,0:T(8,128)(2,1)} %vs_ref.3) | copy-start | bytes 1179652
  37.9 9.3 %copy-start.3 = (bf16[1,256,768]{2,1,0:T(8,128)(2,1)S(1)}, bf16[1,256,768]{2,1,0:T(8,128)(2,1)}, u32[]{:S(2)}) copy-start(bf16[1,256,768]{2,1,0:T(8,128)(2,1)} %ks_ref.3) | copy-start | bytes 1179652
  37.9 9.3 %copy-start.16 = (f32[6,512]{1,0:T(8,128)S(1)}, f32[6,512]{1,0:T(8,128)}, u32[]{:S(2)}) copy-start(f32[6,512]{1,0:T(8,128)} %bias_ref.1) | copy-start | bytes 36868
  40.1 29.3 %copy-start.1 = (bf16[1,256,768]{2,1,0:T(8,128)(2,1)S(1)}, bf16[1,256,768]{2,1,0:T(8,128)(2,1)}, u32[]{:S(2)}) copy-start(bf16[1,256,768]{2,1,0:T(8,128)(2,1)} %cot_ref.3) | copy-start | bytes 1179652
  40.1 29.3 %all-to-all-start.1 = ((bf16[64,8,768]{2,1,0:T(8,128)(2,1)}), bf16[64,8,768]{2,1,0:T(8,128)(2,1)S(1)}, u32[]{:S(2)}, u32[]{:S(2)}) async-start(bf16[64,8,768]{2,1,0:T(8,128)(2,1)} %reorder.1), calls=%async_computation.1 | async-start | bytes 1572864 | tf_op jit(solution)/shard_map/all_to_all | solution.py:362
  51.3 1.2 %copy-start.4 = (f32[6,256,256]{2,1,0:T(8,128)}, f32[6,256,256]{2,1,0:T(8,128)S(1)}, u32[]{:S(2)}) copy-start(f32[6,256,256]{2,1,0:T(8,128)S(1)} %get-tuple-element.26.mem_bias_ref) | copy-start | bytes 4718596
  52.4 0.9 copy-start.11
  53.3 0.9 copy-start.13
  54.2 0.9 copy-start.14
  69.4 1.1 %copy-start.12 = (f32[256,768]{1,0:T(8,128)S(1)}, f32[256,768]{1,0:T(8,128)}, u32[]{:S(2)}) copy-start(f32[256,768]{1,0:T(8,128)} %copy-done.11) | copy-start | bytes 2359300
  74.4 0.9 copy-start.5
  75.3 0.9 copy-start.6
  76.2 3.6 %collective-permute-start.2 = (f32[8,256]{1,0:T(8,128)S(1)}, f32[8,256]{1,0:T(8,128)S(1)}, u32[]{:S(2)}, u32[]{:S(2)}) collective-permute-start(f32[8,256]{1,0:T(8,128)S(1)} %get-tuple-element.30.stats0_ref), channel_id=1, source_target_pairs={{0,3},{1,0},{2,1},{3,2},{4,7},{5,4},{6,5},{7,6},{8,11},{9,8},{10,9... | collective-permute-start | bytes 24584 | tf_op jit(solution)/shard_map/ppermute | solution.py:382
  78.7 4.0 %collective-permute-start.1 = (f32[8,256]{1,0:T(8,128)S(1)}, f32[8,256]{1,0:T(8,128)S(1)}, u32[]{:S(2)}, u32[]{:S(2)}) collective-permute-start(f32[8,256]{1,0:T(8,128)S(1)} %get-tuple-element.30.stats0_ref), channel_id=1, source_target_pairs={{0,2},{1,3},{2,0},{3,1},{4,6},{5,7},{6,4},{7,5},{8,10},{9,11},{10,... | collective-permute-start | bytes 24584 | tf_op jit(solution)/shard_map/ppermute | solution.py:382
  79.2 3.7 %collective-permute-start = (f32[8,256]{1,0:T(8,128)S(1)}, f32[8,256]{1,0:T(8,128)S(1)}, u32[]{:S(2)}, u32[]{:S(2)}) collective-permute-start(f32[8,256]{1,0:T(8,128)S(1)} %get-tuple-element.30.stats0_ref), channel_id=1, source_target_pairs={{0,1},{1,2},{2,3},{3,0},{4,5},{5,6},{6,7},{7,4},{8,9},{9,10},{10,1... | collective-permute-start | bytes 24584 | tf_op jit(solution)/shard_map/ppermute | solution.py:382
  88.1 0.9 copy-start.7
  89.0 0.9 copy-start.9
  90.0 0.7 copy-start.15
  90.6 18.4 %all-to-all-start.2 = ((bf16[64,8,128]{2,1,0:T(8,128)(2,1)}), bf16[64,8,128]{2,1,0:T(8,128)(2,1)}, u32[]{:S(2)}, u32[]{:S(2)}) async-start(bf16[64,8,128]{2,1,0:T(8,128)(2,1)} %copy-done.15), calls=%async_computation.2 | async-start | bytes 262144 | tf_op jit(solution)/shard_map/all_to_all | solution.py:362
  98.7 1.1 %copy-start.8 = (bf16[6,256,256]{2,1,0:T(8,128)(2,1)S(1)}, bf16[6,256,256]{2,1,0:T(8,128)(2,1)}, u32[]{:S(2)}) copy-start(bf16[6,256,256]{2,1,0:T(8,128)(2,1)} %copy-done.7) | copy-start | bytes 2359300
  99.9 1.1 %copy-start.10 = (bf16[6,256,256]{2,1,0:T(8,128)(2,1)S(1)}, bf16[6,256,256]{2,1,0:T(8,128)(2,1)}, u32[]{:S(2)}) copy-start(bf16[6,256,256]{2,1,0:T(8,128)(2,1)} %copy-done.9) | copy-start | bytes 2359300

commit v2 on v1

v2 whole, which is shorter than its diff:
```python
import math

import jax
import jax.numpy as jnp
from jax import lax
from jax.experimental import pallas as pl
from jax.experimental.pallas import tpu as pltpu
from jax.sharding import PartitionSpec as P

DH = 128
BLOCK = 128
HD = 3072
SEG = 256
MEM = 256
POS = 512
HEADS = 6
COLS = HEADS * DH
DP = 64
PIECE = (2 * MEM) // DP
LOG2E = math.log2(math.e)
SCALE = DH ** (-0.5)
FACTOR = SCALE * LOG2E
GROUP = 3
CHUNK = 16
LIMIT = 16
NT = (((1,), (1,)), ((), ()))
NN = (((1,), (0,)), ((), ()))
TN = (((0,), (0,)), ((), ()))


def dot(a, b, dims):
    return lax.dot_general(a, b, dims, preferred_element_type=jnp.float32)


def roll(x, shift):
    shift = shift % x.shape[1]
    return x if shift == 0 else pltpu.roll(x, shift, axis=1)


def reverse_lanes(x):
    rows, width = x.shape
    index = 127 - lax.broadcasted_iota(jnp.int32, (rows, 128), 1)
    parts = [
        jnp.take_along_axis(x[:, start : start + 128], index, axis=1)
        for start in range(width - 128, -1, -128)
    ]
    return jnp.concatenate(parts, axis=1)


def by_distance(x):
    return roll(reverse_lanes(x), -255)


def stagger(x, unit):
    row = lax.broadcasted_iota(jnp.int32, x.shape, 0)
    for bit in (1, 2, 4):
        x = jnp.where((row & bit) != 0, roll(x, bit * unit), x)
    return x


def bias_rows(table, head):
    base = stagger(jnp.broadcast_to(table[head : head + 1], (8, POS)), 1)
    return jnp.concatenate([roll(base, 8 * group) for group in range(SEG // 8)], axis=0)


def diagonal_row(score_grad):
    level = [score_grad[8 * g : 8 * g + 8] for g in range(SEG // 8)]
    while len(level) > 1:
        half = len(level) // 2
        level = [level[k] + roll(level[k + half], -8 * half) for k in range(half)]
    return jnp.sum(stagger(level[0], -1), axis=0, keepdims=True)


def reorder_kernel(owner_ref, in_ref, out_ref, held_ref, source_ref, sem):
    for slot in range(DP):
        source_ref[owner_ref[slot]] = slot
    copies = []
    for part in range(DP // CHUNK):
        for dest in range(CHUNK * part, CHUNK * part + CHUNK):
            held_ref[dest] = in_ref[source_ref[dest]]
        rows = pl.ds(CHUNK * part, CHUNK)
        copy = pltpu.make_async_copy(held_ref.at[rows], out_ref.at[rows], sem.at[part])
        copy.start()
        copies.append(copy)
    for copy in copies:
        copy.wait()


def reorder(new_owner, pieces):
    return pl.pallas_call(
        reorder_kernel,
        out_shape=pltpu.HBM(pieces.shape, pieces.dtype),
        in_specs=[
            pl.BlockSpec(memory_space=pltpu.SMEM),
            pl.BlockSpec(memory_space=pltpu.VMEM),
        ],
        out_specs=pl.BlockSpec(memory_space=pl.ANY),
        scratch_shapes=[
            pltpu.VMEM(pieces.shape, pieces.dtype),
            pltpu.SMEM((DP,), jnp.int32),
            pltpu.SemaphoreType.DMA((DP // CHUNK,)),
        ],
        name="reorder",
    )(new_owner, near(pieces))


def segment_kernel(
    kept_ref, q_ref, ks_ref, vs_ref, bias_ref, prob_ref, out_ref, row_ref, mem_bias_ref
):
    col = lax.broadcasted_iota(jnp.int32, (SEG, SEG), 1)
    row = lax.broadcasted_iota(jnp.int32, (SEG, SEG), 0)
    lane = lax.broadcasted_iota(jnp.int32, (SEG, DH), 1)
    rows = jnp.zeros((SEG, DH), jnp.float32)
    ones = jnp.ones((SEG, DH), jnp.bfloat16)
    seen = col >= MEM - BLOCK * kept_ref[0]
    table = by_distance(bias_ref[...] * LOG2E)
    for g in range(HEADS):
        cols = slice(DH * g, DH * g + DH)
        bias = bias_rows(table, g)
        mem_bias_ref[g] = jnp.where(seen, bias[:, :MEM], -1e30)
        scores = dot(q_ref[0, :, cols], ks_ref[0, :, cols], NT) * FACTOR
        scores = jnp.where(col <= row, scores + bias[:, MEM:], -1e30)
        top = jnp.max(scores, axis=1, keepdims=True)
        prob = jnp.exp2(scores - top).astype(jnp.bfloat16)
        prob_ref[g] = prob
        both = dot(prob, jnp.concatenate([vs_ref[0, :, cols], ones], axis=1), NN)
        out_ref[g] = both[:, :DH]
        rows = jnp.where(lane == g, top, jnp.where(lane == 8 + g, both[:, DH:], rows))
    row_ref[...] = rows


def forward_kernel(
    q_ref, mem_ref, gain_ref, mem_bias_ref, seg_row_ref, seg_out_hbm, cot_hbm,
    out_ref, prob_ref, factor_mem_ref, factor_seg_ref, stats_ref,
    seg_out_ref, cot_ref, sem,
):
    copies = (
        pltpu.make_async_copy(seg_out_hbm, seg_out_ref, sem.at[0]),
        pltpu.make_async_copy(cot_hbm.at[0], cot_ref, sem.at[1]),
    )
    for copy in copies:
        copy.start()
    ones = jnp.ones((MEM, DH), jnp.bfloat16)
    seg_row = seg_row_ref[...]
    for g in range(HEADS):
        cols = slice(DH * g, DH * g + DH)
        scores = dot(q_ref[0, :, cols], mem_ref[:MEM, cols], NT) * FACTOR + mem_bias_ref[g]
        seg_top = jnp.broadcast_to(seg_row[:, g : g + 1], (SEG, DH))
        seg_total = jnp.broadcast_to(seg_row[:, 8 + g : 9 + g], (SEG, DH))
        top = jnp.maximum(jnp.max(scores, axis=1, keepdims=True), seg_top)
        prob = jnp.exp2(scores - jnp.concatenate([top, top], axis=1)).astype(jnp.bfloat16)
        prob_ref[g] = prob
        both = dot(prob, jnp.concatenate([mem_ref[MEM:, cols], ones], axis=1), NN)
        shrink = jnp.exp2(seg_top - top)
        inverse = 1.0 / (both[:, DH:] + seg_total * shrink)
        factor_mem_ref[:, cols] = inverse
        factor_seg_ref[:, cols] = shrink * inverse
        out_ref[:, cols] = both[:, :DH] * inverse
    for copy in copies:
        copy.wait()
    square = cross = None
    for g in range(HEADS):
        cols = slice(DH * g, DH * g + DH)
        out = out_ref[:, cols] + seg_out_ref[g] * factor_seg_ref[:, cols]
        out_ref[:, cols] = out
        part = cot_ref[:, cols].astype(jnp.float32) * gain_ref[:, cols] * out
        square = out * out if g == 0 else square + out * out
        cross = part if g == 0 else cross + part
    stats_ref[...] = jnp.zeros((8, SEG), jnp.float32)
    stats_ref[0:1, :] = jnp.sum(square.T, axis=0, keepdims=True)
    stats_ref[1:2, :] = jnp.sum(cross.T, axis=0, keepdims=True)


def score_grad_kernel(
    stats0_ref, stats1_ref, stats2_ref, stats3_ref,
    vs_ref, mem_ref, cot_ref, gain_ref, attn_ref, prob_mem_ref, prob_seg_ref,
    factor_mem_ref, factor_seg_ref,
    attended_hbm, ds_mem_ref, ds_seg_ref, og_seg_ref, share_ref,
    attended_ref, sem,
):
    stats = (stats0_ref[...] + stats1_ref[...]) + (stats2_ref[...] + stats3_ref[...])
    inv = lax.rsqrt(stats[0:1] / HD + 1e-06)
    coef = inv * inv * inv * stats[1:2] / HD
    inv = jnp.broadcast_to(inv, (DH, SEG)).T
    coef = jnp.broadcast_to(coef, (DH, SEG)).T
    for g in range(HEADS):
        cols = slice(DH * g, DH * g + DH)
        attended_ref[:, cols] = (attn_ref[:, cols] * inv * gain_ref[:, cols]).astype(jnp.bfloat16)
    copy = pltpu.make_async_copy(attended_ref, attended_hbm.at[0], sem)
    copy.start()
    gains = []
    diagonals = []
    for g in range(HEADS):
        cols = slice(DH * g, DH * g + DH)
        attn = attn_ref[:, cols]
        gain = gain_ref[:, cols]
        upstream = cot_ref[0, :, cols].astype(jnp.float32)
        normed = attn * inv
        gains.append(jnp.sum(upstream * normed, axis=0, keepdims=True))
        out_grad = inv * (upstream * gain) - attn * coef
        delta = jnp.sum(out_grad * attn, axis=1, keepdims=True)
        factor_mem = factor_mem_ref[:, cols]
        factor_seg = factor_seg_ref[:, cols]
        og_mem = (out_grad * factor_mem).astype(jnp.bfloat16)
        og_seg = (out_grad * factor_seg).astype(jnp.bfloat16)
        og_seg_ref[g] = og_seg
        less_mem = delta * factor_mem
        less_seg = delta * factor_seg
        dp_mem = dot(og_mem, mem_ref[MEM:, cols], NT) - jnp.concatenate([less_mem, less_mem], axis=1)
        dp_seg = dot(og_seg, vs_ref[0, :, cols], NT) - jnp.concatenate([less_seg, less_seg], axis=1)
        ds_mem = prob_mem_ref[g].astype(jnp.float32) * dp_mem
        ds_seg = prob_seg_ref[g].astype(jnp.float32) * dp_seg
        ds_mem_ref[g] = ds_mem.astype(jnp.bfloat16)
        ds_seg_ref[g] = ds_seg.astype(jnp.bfloat16)
        diagonals.append(diagonal_row(jnp.concatenate([ds_mem, ds_seg], axis=1)))

    pad = [jnp.zeros((2, DH), jnp.float32)]
    gains = jnp.concatenate(gains + pad, axis=0)
    diagonals = jnp.concatenate(diagonals + [jnp.zeros((2, POS), jnp.float32)], axis=0)
    bias = stagger(by_distance(diagonals), 8)
    bias = jnp.concatenate([bias, bias[:, :128]], axis=1)
    lane = lax.broadcasted_iota(jnp.int32, (8, DH), 1)
    row = lax.broadcasted_iota(jnp.int32, (8, DH), 0)
    own = (lane >= 8 * row) & (lane < 8 * row + 8) & (row < HEADS)
    for dest in range(DP):
        start, shift = divmod(8 * dest, 128)
        here = bias[:, 128 * start : 128 * start + 128]
        after = bias[:, 128 * start + 128 : 128 * start + 256]
        part = jnp.where(lane < 128 - shift, roll(here, -shift), roll(after, -shift))
        part = jnp.sum(jnp.where(own, part, 0.0), axis=0, keepdims=True)
        share_ref[dest] = jnp.where(row == HEADS, part, gains).astype(share_ref.dtype)
    copy.wait()


def input_grad_kernel(
    q_ref, ks_ref, mem_ref, ds_mem_ref, ds_seg_ref, prob_seg_ref, og_seg_ref,
    dq_ref, dk_ref, dv_ref,
):
    for g in range(GROUP):
        cols = slice(DH * g, DH * g + DH)
        ds_seg = ds_seg_ref[g]
        dq = dot(ds_mem_ref[g], mem_ref[:, cols], NN) + dot(ds_seg, ks_ref[0, :, cols], NN)
        dq_ref[0, :, cols] = (dq * SCALE).astype(jnp.bfloat16)
        dk_ref[0, :, cols] = (dot(ds_seg, q_ref[0, :, cols], TN) * SCALE).astype(jnp.bfloat16)
        dv_ref[0, :, cols] = dot(prob_seg_ref[g], og_seg_ref[g], TN).astype(jnp.bfloat16)


TOKENS = jax.ShapeDtypeStruct((1, SEG, COLS), jnp.bfloat16)
COLUMNS = jax.ShapeDtypeStruct((SEG, COLS), jnp.float32)
HEAD_COLUMNS = jax.ShapeDtypeStruct((HEADS, SEG, DH), jnp.float32)
HEAD_COLUMNS_B = jax.ShapeDtypeStruct((HEADS, SEG, DH), jnp.bfloat16)
ROWS = jax.ShapeDtypeStruct((SEG, DH), jnp.float32)
STATS = jax.ShapeDtypeStruct((8, SEG), jnp.float32)
SHARES = jax.ShapeDtypeStruct((DP, 8, DH), jnp.bfloat16)
SQUARES = jax.ShapeDtypeStruct((HEADS, SEG, SEG), jnp.float32)
SQUARES_B = jax.ShapeDtypeStruct((HEADS, SEG, SEG), jnp.bfloat16)


def far(x):
    return pltpu.with_memory_space_constraint(x, pltpu.HBM)


def far_out(shape):
    return pltpu.HBM(shape.shape, shape.dtype)


def near(x):
    return pltpu.with_memory_space_constraint(x, pltpu.VMEM)


def near_out(shape):
    return pltpu.VMEM(shape.shape, shape.dtype)


def near_call(kernel, scalars, ins, far_ins, outs, far_outs, tail=(), scratch=()):
    spec = pl.BlockSpec(memory_space=pltpu.VMEM)
    any_spec = pl.BlockSpec(memory_space=pl.ANY)
    return pl.pallas_call(
        kernel,
        in_specs=[pl.BlockSpec(memory_space=pltpu.SMEM)] * len(scalars)
        + [spec] * len(ins)
        + [any_spec] * len(far_ins),
        out_shape=tuple(far_out(x) for x in far_outs) + tuple(outs) + tuple(tail),
        out_specs=(any_spec,) * len(far_outs) + (spec,) * (len(outs) + len(tail)),
        scratch_shapes=scratch,
        compiler_params=pltpu.CompilerParams(vmem_limit_bytes=LIMIT << 20),
        name=kernel.__name__,
    )(*scalars, *[near(x) for x in ins], *[far(x) for x in far_ins])


def segment(kept, q, ks, vs, bias):
    return near_call(
        segment_kernel, (kept,), (q, ks, vs, bias), (),
        [far_out(SQUARES_B), far_out(HEAD_COLUMNS), near_out(ROWS), near_out(SQUARES)], (),
    )


def forward(q, mem, gain, mem_bias, seg_row, seg_out, cot):
    return near_call(
        forward_kernel,
        (),
        (q, mem, gain, mem_bias, seg_row),
        (seg_out, cot),
        [near_out(x) for x in (COLUMNS, SQUARES_B, COLUMNS, COLUMNS, STATS)],
        (),
        scratch=[
            pltpu.VMEM((HEADS, SEG, DH), jnp.float32),
            pltpu.VMEM((SEG, COLS), jnp.bfloat16),
            pltpu.SemaphoreType.DMA((2,)),
        ],
    )


def score_grad(stats, vs, mem, cot, gain, attn, prob_mem, prob_seg, factor_mem, factor_seg):
    return near_call(
        score_grad_kernel,
        (),
        (*stats, vs, mem, cot, gain, attn, prob_mem, prob_seg, factor_mem, factor_seg),
        (),
        [near_out(x) for x in (SQUARES_B, SQUARES_B, HEAD_COLUMNS_B)] + [far_out(SHARES)],
        (TOKENS,),
        scratch=[
            pltpu.VMEM((SEG, COLS), jnp.bfloat16),
            pltpu.SemaphoreType.DMA,
        ],
    )


def input_grad(q, ks, mem, ds_mem, ds_seg, prob_seg, og_seg):
    tokens = pl.BlockSpec((1, SEG, DH * GROUP), lambda h: (0, 0, h))
    squares = pl.BlockSpec((GROUP, SEG, SEG), lambda h: (h, 0, 0))
    return pl.pallas_call(
        input_grad_kernel,
        grid=(HEADS // GROUP,),
        in_specs=[
            tokens,
            tokens,
            pl.BlockSpec((MEM, DH * GROUP), lambda h: (0, h)),
            squares,
            squares,
            squares,
            pl.BlockSpec((GROUP, SEG, DH), lambda h: (h, 0, 0)),
        ],
        out_shape=tuple(far_out(TOKENS) for _ in range(3)),
        out_specs=(tokens,) * 3,
        compiler_params=pltpu.CompilerParams(vmem_limit_bytes=LIMIT << 20),
        name="input_grad_kernel",
    )(far(q), far(ks), near(mem), near(ds_mem), near(ds_seg), far(prob_seg), near(og_seg))


def collect_kernel(share_ref, bias_ref, gain_ref):
    total = jnp.sum(share_ref[...].astype(jnp.float32), axis=0)
    gain_ref[...] = total[:HEADS]
    bias = stagger(jnp.broadcast_to(total[HEADS : HEADS + 1], (8, DH)), -8)
    bias_ref[...] = bias[:HEADS, :8]


def collect(shares):
    return pl.pallas_call(
        collect_kernel,
        in_specs=[pl.BlockSpec(memory_space=pltpu.VMEM)],
        out_shape=(
            pltpu.HBM((HEADS, 8), jnp.float32),
            pltpu.HBM((HEADS, DH), jnp.float32),
        ),
        name="collect",
    )(near(shares))


def exchange(x):
    return lax.all_to_all(x, "dp", split_axis=0, concat_axis=0, tiled=True)


def body(
    seg_queries, seg_keys, seg_values, memory_keys, memory_values,
    new_owner, kept_blocks, rel_bias, norm_gain, cotangent,
):
    own_index = lax.axis_index("dp")
    kept = jnp.sum(jnp.where(new_owner == own_index, kept_blocks, 0)).reshape(1)
    gain = norm_gain.reshape(1, COLS)
    pieces = jnp.concatenate([memory_keys[0], memory_values[0]], axis=0)
    spread = exchange(pieces.reshape(DP, PIECE, COLS))
    mem = exchange(reorder(new_owner, spread)).reshape(2 * MEM, COLS)
    bias = jnp.pad(rel_bias, ((0, 8 - HEADS), (0, 0)))
    prob_seg, seg_out, seg_row, mem_bias = segment(
        kept, seg_queries, seg_keys, seg_values, bias
    )
    attn, prob_mem, factor_mem, factor_seg, stats = forward(
        seg_queries, mem, gain, mem_bias, seg_row, seg_out, cotangent
    )
    others = [
        lax.ppermute(stats, "mp", [(i, (i + step) % 4) for i in range(4)]) for step in (1, 2, 3)
    ]
    attended, ds_mem, ds_seg, og_seg, shares = score_grad(
        [stats] + others, seg_values, mem, cotangent, gain, attn,
        prob_mem, prob_seg, factor_mem, factor_seg,
    )
    query_grad, key_grad, value_grad = input_grad(
        seg_queries, seg_keys, mem, ds_mem, ds_seg, prob_seg, og_seg
    )
    bias_grad, gain_grad = collect(exchange(shares))
    return attended, query_grad, key_grad, value_grad, bias_grad, gain_grad.reshape(COLS)


def solution(mesh):
    row = P("dp", None, "mp")
    return jax.shard_map(
        body,
        mesh=mesh,
        in_specs=(row, row, row, row, row, P(), P(), P("mp", None), P("mp"), row),
        out_specs=(row, row, row, row, P("mp", "dp"), P("mp")),
        check_vma=False,
    )
```

time: 111 us -> 103 us (0.928)
  local copies, waits for them, and re-layouts: 11.6 us -> 3.34 us
  waiting for transfers between devices: 23.1 us -> 26.7 us
  Pallas kernels: 19.5 us -> 16.2 us
    unnamed x40 -> x28, local copies, waits for them, and re-layouts: 11.6 us -> 3.33 us
    all_to_all x2, waiting for transfers between devices: 20 us -> 23.6 us  [exchange(): return lax.all_to_all(x, 'dp', split_axis=0, concat_axis=0, tiled=True)]
    pallas_call x6, Pallas kernels: 19.5 us -> 16.2 us  [the longest x3 10.3 us: near_call(): pl.pallas_call(kernel, in_specs=[pl.BlockSpec(memory_space=pltpu.SMEM)] *...]
  transfers between devices with their start and end apart: 5 -> 5, of which waited for: 4 -> 4; matrix products, arithmetic and copies ran while one was open for 1% -> 1% of each run, Pallas kernels for 6% -> 7%
where the time goes in v2:
time: 103 us
  blocking collectives  35.9 us (35%)
  waiting for transfers between devices  26.7 us (26%)
  starting transfers between devices  17.8 us (17%)
  Pallas kernels  16.2 us (16%)
  local copies, waits for them, and re-layouts  3.34 us (3%)
  other arithmetic  1.8 us (2%)
    all_to_all x1, blocking collectives, exchange(): return lax.all_to_all(x, 'dp', split_axis=0, concat_axis=0, tiled=True)  35.9 us
    all_to_all x2, waiting for transfers between devices, exchange(): return lax.all_to_all(x, 'dp', split_axis=0, concat_axis=0, tiled=True)  23.6 us
    all_to_all x2, starting transfers between devices, exchange(): return lax.all_to_all(x, 'dp', split_axis=0, concat_axis=0, tiled=True)  14.1 us
    pallas_call x3, Pallas kernels, near_call(): pl.pallas_call(kernel, in_specs=[pl.BlockSpec(memory_space=pltpu.SMEM)] *...  10.3 us
    ppermute x3, starting transfers between devices, body(): lax.ppermute(stats, 'mp', [(i, (i + step) % 4) for i in range(4)])  3.67 us
    unnamed x28, local copies, waits for them, and re-layouts  3.33 us
    pallas_call x1, Pallas kernels, input_grad(): pl.pallas_call(input_grad_kernel, grid=(HEADS // GROUP,), in_specs=[token...  3.13 us
    ppermute x3, waiting for transfers between devices, body(): lax.ppermute(stats, 'mp', [(i, (i + step) % 4) for i in range(4)])  3.11 us
  transfers between devices with their start and end apart: 5, of which 4 were waited for; matrix products, arithmetic and copies ran while one was open for 1% of the time, Pallas kernels for 7%

profile of v2, /device:TPU:1, one launch (start us, length us, event | category | flops | bytes accessed | tf_op | source)
XLA Modules:
  0.0 102.5 jit_solution(12070117543150932933)
XLA Ops:
  0.6 1.2 %maximum_bitcast_fusion = bf16[64,8,768]{2,1,0:T(8,128)(2,1)S(1)} fusion(bf16[256,768]{1,0:T(8,128)(2,1)} %bitcast.10, bf16[256,768]{1,0:T(8,128)(2,1)} %bitcast.11), kind=kLoop, calls=%fused_computation | loop fusion | flops 1572864 | bytes 1572864 | tf_op jit(solution)/shard_map/reshape | solution.py:382
  1.8 35.9 %all_to_all.15.in_ref = bf16[64,8,768]{2,1,0:T(8,128)(2,1)S(1)} all-to-all(bf16[64,8,768]{2,1,0:T(8,128)(2,1)S(1)} %maximum_bitcast_fusion), channel_id=1, replica_groups=mesh['dp'=64,'mp'=4] {'dp'}, dimensions={0} | all-to-all | bytes 1572864 | tf_op jit(solution)/shard_map/all_to_all | solution.py:371
  37.7 0.0 copy-start.11
  37.7 0.0 copy-start.10
  37.7 0.0 copy-start.12
  37.7 0.0 copy-start.13
  37.8 0.0 copy-start
  37.8 0.0 copy-start.3
  37.8 0.0 copy-start.5
  37.8 1.8 %reorder.1 = bf16[64,8,768]{2,1,0:T(8,128)(2,1)} custom-call(s32[64]{0:T(128)} %owner_ref.1, bf16[64,8,768]{2,1,0:T(8,128)(2,1)S(1)} %all_to_all.15.in_ref), custom_call_target="tpu_custom_call" | custom-call | tf_op jit(solution)/shard_map/reorder/pallas_call | solution.py:90
  39.6 6.2 %all-to-all-start.1 = ((bf16[64,8,768]{2,1,0:T(8,128)(2,1)}), bf16[64,8,768]{2,1,0:T(8,128)(2,1)S(1)}, u32[]{:S(2)}, u32[]{:S(2)}) async-start(bf16[64,8,768]{2,1,0:T(8,128)(2,1)} %reorder.1), calls=%async_computation.1 | async-start | bytes 1572864 | tf_op jit(solution)/shard_map/all_to_all | solution.py:371
  45.9 0.0 copy-done.11
  45.9 0.0 copy-done.10
  45.9 0.0 copy-done.12
  45.9 0.0 copy-done.13
  45.9 0.6 fusion
  46.6 0.0 copy-done
  46.6 0.0 copy-done.3
  46.6 0.0 copy-done.5
  46.6 4.2 %segment_kernel.1 = (bf16[6,256,256]{2,1,0:T(8,128)(2,1)}, f32[6,256,128]{2,1,0:T(8,128)}, f32[256,128]{1,0:T(8,128)S(1)}, f32[6,256,256]{2,1,0:T(8,128)S(1)}) custom-call(s32[1]{0:T(128)} %bitcast.4.kept_ref, bf16[1,256,768]{2,1,0:T(8,128)(2,1)S(1)} %copy-done, bf16[1,256,768]{2,1,0:T(8,128)(2,1)S(1)} %copy-done.5, bf16[1,256,768]{2,1,0:T(8,128)(2,1)S(1)} %copy-done.3, ...), custom_call_target="tpu_custom_call" | custom-call | tf_op jit(solution)/shard_map/segment_kernel/pallas_call | solution.py:278
  50.8 0.0 copy-start.8
  50.8 0.7 copy-done.8
  51.5 17.4 %all-to-all-done.1 = bf16[64,8,768]{2,1,0:T(8,128)(2,1)S(1)} async-done(((bf16[64,8,768]{2,1,0:T(8,128)(2,1)}), bf16[64,8,768]{2,1,0:T(8,128)(2,1)S(1)}, u32[]{:S(2)}, u32[]{:S(2)}) %all-to-all-start.1) | async-done | bytes 786464 | tf_op jit(solution)/shard_map/all_to_all | solution.py:371
  68.8 0.0 copy-start.9
  68.8 0.9 copy-done.9
  69.7 0.0 copy-start.1
  69.7 0.0 copy-start.2
  69.7 0.0 copy-start.4
  69.7 2.6 %forward_kernel.1 = (f32[256,768]{1,0:T(8,128)S(1)}, bf16[6,256,256]{2,1,0:T(8,128)(2,1)S(1)}, f32[256,768]{1,0:T(8,128)S(1)}, f32[256,768]{1,0:T(8,128)S(1)}, f32[8,256]{1,0:T(8,128)S(1)}) custom-call(bf16[1,256,768]{2,1,0:T(8,128)(2,1)S(1)} %copy-done, bf16[512,768]{1,0:T(8,128)(2,1)S(1)} %bitcast.7, f32[1,768]{1,0:T(1,128)S(1)} %reshape.29.gain_ref, ...), custom_call_target="tpu_custom_call" | custom-call | tf_op jit(solution)/shard_map/forward_kernel/pallas_call | solution.py:278
  72.3 2.6 %collective-permute-start.2 = (f32[8,256]{1,0:T(8,128)S(1)}, f32[8,256]{1,0:T(8,128)S(1)}, u32[]{:S(2)}, u32[]{:S(2)}) collective-permute-start(f32[8,256]{1,0:T(8,128)S(1)} %get-tuple-element.28.stats0_ref), channel_id=1, source_target_pairs={{0,3},{1,0},{2,1},{3,2},{4,7},{5,4},{6,5},{7,6},{8,11},{9,8},{10,9... | collective-permute-start | bytes 24584 | tf_op jit(solution)/shard_map/ppermute | solution.py:392
  74.9 0.5 collective-permute-start.1
  75.4 0.6 collective-permute-start
  76.0 0.0 collective-permute-done.2.stats3_ref
  76.0 2.9 %collective-permute-done.1.stats2_ref = f32[8,256]{1,0:T(8,128)S(1)} collective-permute-done((f32[8,256]{1,0:T(8,128)S(1)}, f32[8,256]{1,0:T(8,128)S(1)}, u32[]{:S(2)}, u32[]{:S(2)}) %collective-permute-start.1) | collective-permute-done | bytes 8224 | tf_op jit(solution)/shard_map/ppermute | solution.py:392
  78.9 0.2 collective-permute-done.stats1_ref
  79.1 0.0 copy-done.1
  79.1 0.0 copy-done.2
  79.1 0.0 copy-done.4
  79.1 3.5 %score_grad_kernel.1 = (bf16[1,256,768]{2,1,0:T(8,128)(2,1)}, bf16[6,256,256]{2,1,0:T(8,128)(2,1)S(1)}, bf16[6,256,256]{2,1,0:T(8,128)(2,1)S(1)}, bf16[6,256,128]{2,1,0:T(8,128)(2,1)S(1)}, bf16[64,8,128]{2,1,0:T(8,128)(2,1)}) custom-call(f32[8,256]{1,0:T(8,128)S(1)} %get-tuple-element.28.stats0_ref, f32[8,256]{1,0:T(8,128)S(1)} %collective-permute-done.stats1_ref, ...), custom_call_target="tpu_custom_call" | custom-call | tf_op jit(solution)/shard_map/score_grad_kernel/pallas_call | solution.py:278
  82.6 0.0 copy-start.6
  82.6 0.7 copy-done.6
  83.4 7.9 %all-to-all-start.2 = ((bf16[64,8,128]{2,1,0:T(8,128)(2,1)}), bf16[64,8,128]{2,1,0:T(8,128)(2,1)S(1)}, u32[]{:S(2)}, u32[]{:S(2)}) async-start(bf16[64,8,128]{2,1,0:T(8,128)(2,1)} %get-tuple-element.41), calls=%async_computation.2 | async-start | bytes 262144 | tf_op jit(solution)/shard_map/all_to_all | solution.py:371
  91.3 0.0 copy-start.7
  91.3 1.0 copy-done.7
  92.3 3.1 %input_grad_kernel.1 = (bf16[1,256,768]{2,1,0:T(8,128)(2,1)}, bf16[1,256,768]{2,1,0:T(8,128)(2,1)}, bf16[1,256,768]{2,1,0:T(8,128)(2,1)}) custom-call(bf16[1,256,768]{2,1,0:T(8,128)(2,1)} %q_ref.5, bf16[1,256,768]{2,1,0:T(8,128)(2,1)} %ks_ref.3, bf16[512,768]{1,0:T(8,128)(2,1)S(1)} %bitcast.9, bf16[6,256,256]{2,1,0:T(8,128)(2,1)S(1)} %get-tuple-element.35.ds_mem_ref, ...), custom_call_target="tpu_custom_call" | custom-call | tf_op jit(solution)/shard_map/input_grad_kernel/pallas_call | solution.py:332
  95.4 6.2 %all-to-all-done.2.share_ref = bf16[64,8,128]{2,1,0:T(8,128)(2,1)S(1)} async-done(((bf16[64,8,128]{2,1,0:T(8,128)(2,1)}), bf16[64,8,128]{2,1,0:T(8,128)(2,1)S(1)}, u32[]{:S(2)}, u32[]{:S(2)}) %all-to-all-start.2) | async-done | bytes 131104 | tf_op jit(solution)/shard_map/all_to_all | solution.py:371
  101.6 0.9 collect.1
  (2 shorter events, 0.0 us)
Async XLA Ops:
  37.7 8.1 %copy-start.11 = (f32[768]{0:T(1024)S(1)}, f32[768]{0:T(1024)}, u32[]{:S(2)}) copy-start(f32[768]{0:T(1024)} %param.18) | copy-start | bytes 9220
  37.7 8.1 %copy-start.10 = (f32[6,512]{1,0:T(8,128)S(1)}, f32[6,512]{1,0:T(8,128)}, u32[]{:S(2)}) copy-start(f32[6,512]{1,0:T(8,128)} %param.17) | copy-start | bytes 36868
  37.7 8.2 %copy-start.12 = (s32[64]{0:T(128)S(1)}, s32[64]{0:T(128)}, u32[]{:S(2)}) copy-start(s32[64]{0:T(128)} %owner_ref.1) | copy-start | bytes 772
  37.7 8.2 %copy-start.13 = (s32[64]{0:T(128)S(1)}, s32[64]{0:T(128)}, u32[]{:S(2)}) copy-start(s32[64]{0:T(128)} %param.16) | copy-start | bytes 772
  37.8 8.8 %copy-start = (bf16[1,256,768]{2,1,0:T(8,128)(2,1)S(1)}, bf16[1,256,768]{2,1,0:T(8,128)(2,1)}, u32[]{:S(2)}) copy-start(bf16[1,256,768]{2,1,0:T(8,128)(2,1)} %q_ref.5) | copy-start | bytes 1179652
  37.8 8.8 %copy-start.3 = (bf16[1,256,768]{2,1,0:T(8,128)(2,1)S(1)}, bf16[1,256,768]{2,1,0:T(8,128)(2,1)}, u32[]{:S(2)}) copy-start(bf16[1,256,768]{2,1,0:T(8,128)(2,1)} %vs_ref.3) | copy-start | bytes 1179652
  37.8 8.8 %copy-start.5 = (bf16[1,256,768]{2,1,0:T(8,128)(2,1)S(1)}, bf16[1,256,768]{2,1,0:T(8,128)(2,1)}, u32[]{:S(2)}) copy-start(bf16[1,256,768]{2,1,0:T(8,128)(2,1)} %ks_ref.3) | copy-start | bytes 1179652
  39.6 29.2 %all-to-all-start.1 = ((bf16[64,8,768]{2,1,0:T(8,128)(2,1)}), bf16[64,8,768]{2,1,0:T(8,128)(2,1)S(1)}, u32[]{:S(2)}, u32[]{:S(2)}) async-start(bf16[64,8,768]{2,1,0:T(8,128)(2,1)} %reorder.1), calls=%async_computation.1 | async-start | bytes 1572864 | tf_op jit(solution)/shard_map/all_to_all | solution.py:371
  50.8 0.7 copy-start.8
  68.8 0.9 copy-start.9
  69.7 9.4 %copy-start.1 = (bf16[6,256,256]{2,1,0:T(8,128)(2,1)S(1)}, bf16[6,256,256]{2,1,0:T(8,128)(2,1)}, u32[]{:S(2)}) copy-start(bf16[6,256,256]{2,1,0:T(8,128)(2,1)} %get-tuple-element.31.prob_seg_ref) | copy-start | bytes 2359300
  69.7 9.4 %copy-start.2 = (bf16[1,256,768]{2,1,0:T(8,128)(2,1)S(1)}, bf16[1,256,768]{2,1,0:T(8,128)(2,1)}, u32[]{:S(2)}) copy-start(bf16[1,256,768]{2,1,0:T(8,128)(2,1)} %cot_ref.1) | copy-start | bytes 1179652
  69.7 9.4 %copy-start.4 = (bf16[1,256,768]{2,1,0:T(8,128)(2,1)S(1)}, bf16[1,256,768]{2,1,0:T(8,128)(2,1)}, u32[]{:S(2)}) copy-start(bf16[1,256,768]{2,1,0:T(8,128)(2,1)} %vs_ref.3) | copy-start | bytes 1179652
  72.3 3.7 %collective-permute-start.2 = (f32[8,256]{1,0:T(8,128)S(1)}, f32[8,256]{1,0:T(8,128)S(1)}, u32[]{:S(2)}, u32[]{:S(2)}) collective-permute-start(f32[8,256]{1,0:T(8,128)S(1)} %get-tuple-element.28.stats0_ref), channel_id=1, source_target_pairs={{0,3},{1,0},{2,1},{3,2},{4,7},{5,4},{6,5},{7,6},{8,11},{9,8},{10,9... | collective-permute-start | bytes 24584 | tf_op jit(solution)/shard_map/ppermute | solution.py:392
  74.9 4.0 %collective-permute-start.1 = (f32[8,256]{1,0:T(8,128)S(1)}, f32[8,256]{1,0:T(8,128)S(1)}, u32[]{:S(2)}, u32[]{:S(2)}) collective-permute-start(f32[8,256]{1,0:T(8,128)S(1)} %get-tuple-element.28.stats0_ref), channel_id=1, source_target_pairs={{0,2},{1,3},{2,0},{3,1},{4,6},{5,7},{6,4},{7,5},{8,10},{9,11},{10,... | collective-permute-start | bytes 24584 | tf_op jit(solution)/shard_map/ppermute | solution.py:392
  75.4 3.7 %collective-permute-start = (f32[8,256]{1,0:T(8,128)S(1)}, f32[8,256]{1,0:T(8,128)S(1)}, u32[]{:S(2)}, u32[]{:S(2)}) collective-permute-start(f32[8,256]{1,0:T(8,128)S(1)} %get-tuple-element.28.stats0_ref), channel_id=1, source_target_pairs={{0,1},{1,2},{2,3},{3,0},{4,5},{5,6},{6,7},{7,4},{8,9},{9,10},{10,1... | collective-permute-start | bytes 24584 | tf_op jit(solution)/shard_map/ppermute | solution.py:392
  82.6 0.7 copy-start.6
  83.4 18.3 %all-to-all-start.2 = ((bf16[64,8,128]{2,1,0:T(8,128)(2,1)}), bf16[64,8,128]{2,1,0:T(8,128)(2,1)S(1)}, u32[]{:S(2)}, u32[]{:S(2)}) async-start(bf16[64,8,128]{2,1,0:T(8,128)(2,1)} %get-tuple-element.41), calls=%async_computation.2 | async-start | bytes 262144 | tf_op jit(solution)/shard_map/all_to_all | solution.py:371
  91.3 1.0 copy-start.7

commit v3 on v2

--- a/solution.py
+++ b/solution.py
@@ -11,6 +11,7 @@
 BLOCK = 128
 HD = 3072
 SEG = 256
+HALF = SEG // 2
 MEM = 256
 POS = 512
 HEADS = 6
@@ -105,19 +106,20 @@
 
 
 def segment_kernel(
-    kept_ref, q_ref, ks_ref, vs_ref, bias_ref, prob_ref, out_ref, row_ref, mem_bias_ref
+    q_ref, ks_ref, vs_ref, bias_ref, gain_ref, prob_ref, out_ref, table_ref
 ):
     col = lax.broadcasted_iota(jnp.int32, (SEG, SEG), 1)
     row = lax.broadcasted_iota(jnp.int32, (SEG, SEG), 0)
     lane = lax.broadcasted_iota(jnp.int32, (SEG, DH), 1)
     rows = jnp.zeros((SEG, DH), jnp.float32)
     ones = jnp.ones((SEG, DH), jnp.bfloat16)
-    seen = col >= MEM - BLOCK * kept_ref[0]
     table = by_distance(bias_ref[...] * LOG2E)
     for g in range(HEADS):
         cols = slice(DH * g, DH * g + DH)
         bias = bias_rows(table, g)
-        mem_bias_ref[g] = jnp.where(seen, bias[:, :MEM], -1e30)
+        table_ref[HALF * g : HALF * g + HALF] = jnp.concatenate(
+            [bias[HALF:, :DH], bias[:HALF, :MEM]], axis=1
+        )
         scores = dot(q_ref[0, :, cols], ks_ref[0, :, cols], NT) * FACTOR
         scores = jnp.where(col <= row, scores + bias[:, MEM:], -1e30)
         top = jnp.max(scores, axis=1, keepdims=True)
@@ -126,11 +128,14 @@
         both = dot(prob, jnp.concatenate([vs_ref[0, :, cols], ones], axis=1), NN)
         out_ref[g] = both[:, :DH]
         rows = jnp.where(lane == g, top, jnp.where(lane == 8 + g, both[:, DH:], rows))
-    row_ref[...] = rows
+    table_ref[HALF * HEADS : HALF * HEADS + 16, :SEG] = rows.T[:16]
+    for g in range(0, HEADS, 3):
+        row = HALF * HEADS + 16 + g // 3
+        table_ref[row : row + 1] = gain_ref[:, DH * g : DH * g + 3 * DH]
 
 
 def forward_kernel(
-    q_ref, mem_ref, gain_ref, mem_bias_ref, seg_row_ref, seg_out_hbm, cot_hbm,
+    kept_ref, q_ref, mem_ref, table_ref, seg_out_hbm, cot_hbm,
     out_ref, prob_ref, factor_mem_ref, factor_seg_ref, stats_ref,
     seg_out_ref, cot_ref, sem,
 ):
@@ -141,12 +146,16 @@
     for copy in copies:
         copy.start()
     ones = jnp.ones((MEM, DH), jnp.bfloat16)
-    seg_row = seg_row_ref[...]
+    seg_row = table_ref[HALF * HEADS : HALF * HEADS + 16, :SEG]
+    both_kept = jnp.full((SEG, BLOCK), kept_ref[0], jnp.int32) > 1
     for g in range(HEADS):
         cols = slice(DH * g, DH * g + DH)
-        scores = dot(q_ref[0, :, cols], mem_ref[:MEM, cols], NT) * FACTOR + mem_bias_ref[g]
-        seg_top = jnp.broadcast_to(seg_row[:, g : g + 1], (SEG, DH))
-        seg_total = jnp.broadcast_to(seg_row[:, 8 + g : 9 + g], (SEG, DH))
+        scores = dot(q_ref[0, :, cols], mem_ref[:MEM, cols], NT) * FACTOR
+        bias = table_ref[HALF * g : HALF * g + HALF]
+        scores = scores + jnp.concatenate([bias[:, DH:], bias[:, :MEM]], axis=0)
+        scores = jnp.concatenate([jnp.where(both_kept, scores[:, :BLOCK], -1e30), scores[:, BLOCK:]], axis=1)
+        seg_top = jnp.broadcast_to(seg_row[g : g + 1], (DH, SEG)).T
+        seg_total = jnp.broadcast_to(seg_row[8 + g : 9 + g], (DH, SEG)).T
         top = jnp.maximum(jnp.max(scores, axis=1, keepdims=True), seg_top)
         prob = jnp.exp2(scores - jnp.concatenate([top, top], axis=1)).astype(jnp.bfloat16)
         prob_ref[g] = prob
@@ -163,7 +172,9 @@
         cols = slice(DH * g, DH * g + DH)
         out = out_ref[:, cols] + seg_out_ref[g] * factor_seg_ref[:, cols]
         out_ref[:, cols] = out
-        part = cot_ref[:, cols].astype(jnp.float32) * gain_ref[:, cols] * out
+        row = HALF * HEADS + 16 + g // 3
+        gain = table_ref[row : row + 1, DH * (g % 3) : DH * (g % 3) + DH]
+        part = cot_ref[:, cols].astype(jnp.float32) * gain * out
         square = out * out if g == 0 else square + out * out
         cross = part if g == 0 else cross + part
     stats_ref[...] = jnp.zeros((8, SEG), jnp.float32)
@@ -173,41 +184,51 @@
 
 def score_grad_kernel(
     stats0_ref, stats1_ref, stats2_ref, stats3_ref,
-    vs_ref, mem_ref, cot_ref, gain_ref, attn_ref, prob_mem_ref, prob_seg_ref,
-    factor_mem_ref, factor_seg_ref,
-    attended_hbm, ds_mem_ref, ds_seg_ref, og_seg_ref, share_ref,
-    attended_ref, sem,
+    mem_ref, cot_ref, gain_ref, attn_ref, prob_mem_ref, prob_seg_ref,
+    factor_mem_ref, factor_seg_ref, vs_hbm,
+    attended_hbm, og_seg_hbm, keys_hbm, ds_mem_ref, ds_seg_ref, share_ref,
+    attended_ref, og_seg_ref, og_mem_ref, less_ref, vs_ref, sem,
 ):
+    values_copy = pltpu.make_async_copy(vs_hbm.at[0], vs_ref, sem.at[0])
+    values_copy.start()
+    keys_copy = pltpu.make_async_copy(mem_ref.at[pl.ds(0, MEM)], keys_hbm, sem.at[1])
+    keys_copy.start()
     stats = (stats0_ref[...] + stats1_ref[...]) + (stats2_ref[...] + stats3_ref[...])
     inv = lax.rsqrt(stats[0:1] / HD + 1e-06)
     coef = inv * inv * inv * stats[1:2] / HD
     inv = jnp.broadcast_to(inv, (DH, SEG)).T
     coef = jnp.broadcast_to(coef, (DH, SEG)).T
-    for g in range(HEADS):
-        cols = slice(DH * g, DH * g + DH)
-        attended_ref[:, cols] = (attn_ref[:, cols] * inv * gain_ref[:, cols]).astype(jnp.bfloat16)
-    copy = pltpu.make_async_copy(attended_ref, attended_hbm.at[0], sem)
-    copy.start()
     gains = []
-    diagonals = []
     for g in range(HEADS):
         cols = slice(DH * g, DH * g + DH)
         attn = attn_ref[:, cols]
         gain = gain_ref[:, cols]
         upstream = cot_ref[0, :, cols].astype(jnp.float32)
         normed = attn * inv
+        attended_ref[:, cols] = (normed * gain).astype(jnp.bfloat16)
         gains.append(jnp.sum(upstream * normed, axis=0, keepdims=True))
         out_grad = inv * (upstream * gain) - attn * coef
-        delta = jnp.sum(out_grad * attn, axis=1, keepdims=True)
-        factor_mem = factor_mem_ref[:, cols]
-        factor_seg = factor_seg_ref[:, cols]
-        og_mem = (out_grad * factor_mem).astype(jnp.bfloat16)
-        og_seg = (out_grad * factor_seg).astype(jnp.bfloat16)
-        og_seg_ref[g] = og_seg
-        less_mem = delta * factor_mem
-        less_seg = delta * factor_seg
-        dp_mem = dot(og_mem, mem_ref[MEM:, cols], NT) - jnp.concatenate([less_mem, less_mem], axis=1)
-        dp_seg = dot(og_seg, vs_ref[0, :, cols], NT) - jnp.concatenate([less_seg, less_seg], axis=1)
+        less_ref[g] = jnp.broadcast_to(
+            jnp.sum(out_grad * attn, axis=1, keepdims=True), (SEG, DH)
+        )
+        og_mem_ref[g] = (out_grad * factor_mem_ref[:, cols]).astype(jnp.bfloat16)
+        og_seg_ref[g] = (out_grad * factor_seg_ref[:, cols]).astype(jnp.bfloat16)
+    copies = (
+        pltpu.make_async_copy(attended_ref, attended_hbm.at[0], sem.at[2]),
+        pltpu.make_async_copy(og_seg_ref, og_seg_hbm, sem.at[3]),
+    )
+    for copy in copies:
+        copy.start()
+    values_copy.wait()
+    diagonals = []
+    for g in range(HEADS):
+        cols = slice(DH * g, DH * g + DH)
+        less_mem = less_ref[g] * factor_mem_ref[:, cols]
+        less_seg = less_ref[g] * factor_seg_ref[:, cols]
+        dp_mem = dot(og_mem_ref[g], mem_ref[MEM:, cols], NT)
+        dp_seg = dot(og_seg_ref[g], vs_ref[:, cols], NT)
+        dp_mem = dp_mem - jnp.concatenate([less_mem, less_mem], axis=1)
+        dp_seg = dp_seg - jnp.concatenate([less_seg, less_seg], axis=1)
         ds_mem = prob_mem_ref[g].astype(jnp.float32) * dp_mem
         ds_seg = prob_seg_ref[g].astype(jnp.float32) * dp_seg
         ds_mem_ref[g] = ds_mem.astype(jnp.bfloat16)
@@ -229,7 +250,9 @@
         part = jnp.where(lane < 128 - shift, roll(here, -shift), roll(after, -shift))
         part = jnp.sum(jnp.where(own, part, 0.0), axis=0, keepdims=True)
         share_ref[dest] = jnp.where(row == HEADS, part, gains).astype(share_ref.dtype)
-    copy.wait()
+    keys_copy.wait()
+    for copy in copies:
+        copy.wait()
 
 
 def input_grad_kernel(
@@ -249,10 +272,10 @@
 COLUMNS = jax.ShapeDtypeStruct((SEG, COLS), jnp.float32)
 HEAD_COLUMNS = jax.ShapeDtypeStruct((HEADS, SEG, DH), jnp.float32)
 HEAD_COLUMNS_B = jax.ShapeDtypeStruct((HEADS, SEG, DH), jnp.bfloat16)
-ROWS = jax.ShapeDtypeStruct((SEG, DH), jnp.float32)
+TABLE = jax.ShapeDtypeStruct((HEADS * HALF + 24, MEM + DH), jnp.float32)
 STATS = jax.ShapeDtypeStruct((8, SEG), jnp.float32)
+KEYS = jax.ShapeDtypeStruct((MEM, COLS), jnp.bfloat16)
 SHARES = jax.ShapeDtypeStruct((DP, 8, DH), jnp.bfloat16)
-SQUARES = jax.ShapeDtypeStruct((HEADS, SEG, SEG), jnp.float32)
 SQUARES_B = jax.ShapeDtypeStruct((HEADS, SEG, SEG), jnp.bfloat16)
 
 
@@ -288,18 +311,25 @@
     )(*scalars, *[near(x) for x in ins], *[far(x) for x in far_ins])
 
 
-def segment(kept, q, ks, vs, bias):
-    return near_call(
-        segment_kernel, (kept,), (q, ks, vs, bias), (),
-        [far_out(SQUARES_B), far_out(HEAD_COLUMNS), near_out(ROWS), near_out(SQUARES)], (),
-    )
-
-
-def forward(q, mem, gain, mem_bias, seg_row, seg_out, cot):
+def segment(q, ks, vs, bias, gain):
+    spec = pl.BlockSpec(memory_space=pltpu.VMEM)
+    return pl.pallas_call(
+        segment_kernel,
+        in_specs=[spec] * 5,
+        out_shape=(
+            far_out(SQUARES_B), far_out(HEAD_COLUMNS), near_out(TABLE),
+        ),
+        out_specs=(spec,) * 3,
+        compiler_params=pltpu.CompilerParams(vmem_limit_bytes=LIMIT << 20),
+        name="segment_kernel",
+    )(far(q), far(ks), far(vs), bias, far(gain))
+
+
+def forward(kept, q, mem, table, seg_out, cot):
     return near_call(
         forward_kernel,
-        (),
-        (q, mem, gain, mem_bias, seg_row),
+        (kept,),
+        (q, mem, table),
         (seg_out, cot),
         [near_out(x) for x in (COLUMNS, SQUARES_B, COLUMNS, COLUMNS, STATS)],
         (),
@@ -315,18 +345,22 @@
     return near_call(
         score_grad_kernel,
         (),
-        (*stats, vs, mem, cot, gain, attn, prob_mem, prob_seg, factor_mem, factor_seg),
-        (),
-        [near_out(x) for x in (SQUARES_B, SQUARES_B, HEAD_COLUMNS_B)] + [far_out(SHARES)],
-        (TOKENS,),
+        (*stats, mem, cot, gain, attn, prob_mem, prob_seg, factor_mem, factor_seg),
+        (vs,),
+        [near_out(SQUARES_B), near_out(SQUARES_B), far_out(SHARES)],
+        (TOKENS, HEAD_COLUMNS_B, KEYS),
         scratch=[
             pltpu.VMEM((SEG, COLS), jnp.bfloat16),
-            pltpu.SemaphoreType.DMA,
+            pltpu.VMEM((HEADS, SEG, DH), jnp.bfloat16),
+            pltpu.VMEM((HEADS, SEG, DH), jnp.bfloat16),
+            pltpu.VMEM((HEADS, SEG, DH), jnp.float32),
+            pltpu.VMEM((SEG, COLS), jnp.bfloat16),
+            pltpu.SemaphoreType.DMA((4,)),
         ],
     )
 
 
-def input_grad(q, ks, mem, ds_mem, ds_seg, prob_seg, og_seg):
+def input_grad(q, ks, keys, ds_mem, ds_seg, prob_seg, og_seg):
     tokens = pl.BlockSpec((1, SEG, DH * GROUP), lambda h: (0, 0, h))
     squares = pl.BlockSpec((GROUP, SEG, SEG), lambda h: (h, 0, 0))
     return pl.pallas_call(
@@ -345,7 +379,7 @@
         out_specs=(tokens,) * 3,
         compiler_params=pltpu.CompilerParams(vmem_limit_bytes=LIMIT << 20),
         name="input_grad_kernel",
-    )(far(q), far(ks), near(mem), near(ds_mem), near(ds_seg), far(prob_seg), near(og_seg))
+    )(far(q), far(ks), far(keys), near(ds_mem), near(ds_seg), far(prob_seg), far(og_seg))
 
 
 def collect_kernel(share_ref, bias_ref, gain_ref):
@@ -382,21 +416,21 @@
     spread = exchange(pieces.reshape(DP, PIECE, COLS))
     mem = exchange(reorder(new_owner, spread)).reshape(2 * MEM, COLS)
     bias = jnp.pad(rel_bias, ((0, 8 - HEADS), (0, 0)))
-    prob_seg, seg_out, seg_row, mem_bias = segment(
-        kept, seg_queries, seg_keys, seg_values, bias
+    prob_seg, seg_out, table = segment(
+        seg_queries, seg_keys, seg_values, bias, gain
     )
     attn, prob_mem, factor_mem, factor_seg, stats = forward(
-        seg_queries, mem, gain, mem_bias, seg_row, seg_out, cotangent
+        kept, seg_queries, mem, table, seg_out, cotangent
     )
     others = [
         lax.ppermute(stats, "mp", [(i, (i + step) % 4) for i in range(4)]) for step in (1, 2, 3)
     ]
-    attended, ds_mem, ds_seg, og_seg, shares = score_grad(
+    attended, og_seg, mem_keys, ds_mem, ds_seg, shares = score_grad(
         [stats] + others, seg_values, mem, cotangent, gain, attn,
         prob_mem, prob_seg, factor_mem, factor_seg,
     )
     query_grad, key_grad, value_grad = input_grad(
-        seg_queries, seg_keys, mem, ds_mem, ds_seg, prob_seg, og_seg
+        seg_queries, seg_keys, mem_keys, ds_mem, ds_seg, prob_seg, og_seg
     )
     bias_grad, gain_grad = collect(exchange(shares))
     return attended, query_grad, key_grad, value_grad, bias_grad, gain_grad.reshape(COLS)

time: 103 us -> 101 us (0.981)
  local copies, waits for them, and re-layouts: 3.34 us -> 0.62 us
    pallas_call x0 -> x1, Pallas kernels: none -> 4.72 us  [segment(): pl.pallas_call(segment_kernel, in_specs=[spec] * 5, out_shape=(far_out(SQ...]
    pallas_call x3 -> x2, Pallas kernels: 10.3 us -> 5.89 us  [near_call(): pl.pallas_call(kernel, in_specs=[pl.BlockSpec(memory_space=pltpu.SMEM)] *...]
    unnamed x28 -> x16, local copies, waits for them, and re-layouts: 3.33 us -> 0.04 us
  transfers between devices with their start and end apart: 5 -> 5, of which waited for: 4 -> 4; matrix products, arithmetic and copies ran while one was open for 1% -> 1% of each run, Pallas kernels for 7% -> 8%
where the time goes in v3:
time: 101 us
  blocking collectives  35.9 us (36%)
  waiting for transfers between devices  27.3 us (27%)
  starting transfers between devices  17.9 us (18%)
  Pallas kernels  16.5 us (16%)
  other arithmetic  1.8 us (2%)
    all_to_all x1, blocking collectives, exchange(): return lax.all_to_all(x, 'dp', split_axis=0, concat_axis=0, tiled=True)  35.9 us
    all_to_all x2, waiting for transfers between devices, exchange(): return lax.all_to_all(x, 'dp', split_axis=0, concat_axis=0, tiled=True)  24.2 us
    all_to_all x2, starting transfers between devices, exchange(): return lax.all_to_all(x, 'dp', split_axis=0, concat_axis=0, tiled=True)  14.2 us
    pallas_call x2, Pallas kernels, near_call(): pl.pallas_call(kernel, in_specs=[pl.BlockSpec(memory_space=pltpu.SMEM)] *...  5.89 us
    pallas_call x1, Pallas kernels, segment(): pl.pallas_call(segment_kernel, in_specs=[spec] * 5, out_shape=(far_out(SQ...  4.72 us
    ppermute x3, starting transfers between devices, body(): lax.ppermute(stats, 'mp', [(i, (i + step) % 4) for i in range(4)])  3.68 us
    pallas_call x1, Pallas kernels, input_grad(): pl.pallas_call(input_grad_kernel, grid=(HEADS // GROUP,), in_specs=[token...  3.22 us
    ppermute x3, waiting for transfers between devices, body(): lax.ppermute(stats, 'mp', [(i, (i + step) % 4) for i in range(4)])  3.1 us
  transfers between devices with their start and end apart: 5, of which 4 were waited for; matrix products, arithmetic and copies ran while one was open for 1% of the time, Pallas kernels for 8%

profile of v3, /device:TPU:1, one launch (start us, length us, event | category | flops | bytes accessed | tf_op | source)
XLA Modules:
  0.0 100.8 jit_solution(17034928919192048597)
XLA Ops:
  0.6 1.2 %maximum_bitcast_fusion = bf16[64,8,768]{2,1,0:T(8,128)(2,1)S(1)} fusion(bf16[256,768]{1,0:T(8,128)(2,1)} %bitcast.9, bf16[256,768]{1,0:T(8,128)(2,1)} %bitcast.10), kind=kLoop, calls=%fused_computation | loop fusion | flops 1572864 | bytes 1572864 | tf_op jit(solution)/shard_map/reshape | solution.py:416
  1.8 35.9 %all_to_all.15.in_ref = bf16[64,8,768]{2,1,0:T(8,128)(2,1)S(1)} all-to-all(bf16[64,8,768]{2,1,0:T(8,128)(2,1)S(1)} %maximum_bitcast_fusion), channel_id=1, replica_groups=mesh['dp'=64,'mp'=4] {'dp'}, dimensions={0} | all-to-all | bytes 1572864 | tf_op jit(solution)/shard_map/all_to_all | solution.py:405
  37.7 0.0 copy-start.5
  37.7 0.0 copy-start.4
  37.7 1.8 %reorder.1 = bf16[64,8,768]{2,1,0:T(8,128)(2,1)} custom-call(s32[64]{0:T(128)} %owner_ref.1, bf16[64,8,768]{2,1,0:T(8,128)(2,1)S(1)} %all_to_all.15.in_ref), custom_call_target="tpu_custom_call" | custom-call | tf_op jit(solution)/shard_map/reorder/pallas_call | solution.py:91
  39.6 0.0 copy-start.6
  39.6 0.0 copy-start.7
  39.6 0.0 copy-start
  39.6 6.3 %all-to-all-start.1 = ((bf16[64,8,768]{2,1,0:T(8,128)(2,1)}), bf16[64,8,768]{2,1,0:T(8,128)(2,1)S(1)}, u32[]{:S(2)}, u32[]{:S(2)}) async-start(bf16[64,8,768]{2,1,0:T(8,128)(2,1)} %reorder.1), calls=%async_computation.1 | async-start | bytes 1572864 | tf_op jit(solution)/shard_map/all_to_all | solution.py:405
  46.0 0.0 copy-done.5
  46.0 0.6 reshape.30.gain_ref
  46.6 0.0 copy-done.4
  46.6 4.7 %segment_kernel.1 = (bf16[6,256,256]{2,1,0:T(8,128)(2,1)}, f32[6,256,128]{2,1,0:T(8,128)}, f32[792,384]{1,0:T(8,128)S(1)}) custom-call(bf16[1,256,768]{2,1,0:T(8,128)(2,1)} %q_ref.5, bf16[1,256,768]{2,1,0:T(8,128)(2,1)} %ks_ref.3, bf16[1,256,768]{2,1,0:T(8,128)(2,1)} %vs_hbm.1, f32[8,512]{1,0:T(8,128)S(1)} %pad.4.bias_ref, f32[1,768]{1,0:T(1,128)} %reshape.30.gain_ref), custom_call_target="tpu_custom_call" | custom-call | tf_op jit(solution)/shard_map/segment_kernel/pallas_call | solution.py:316
  51.3 0.0 copy-done.6
  51.3 0.0 copy-done.7
  51.3 0.6 fusion
  51.9 17.0 %all-to-all-done.1 = bf16[64,8,768]{2,1,0:T(8,128)(2,1)S(1)} async-done(((bf16[64,8,768]{2,1,0:T(8,128)(2,1)}), bf16[64,8,768]{2,1,0:T(8,128)(2,1)S(1)}, u32[]{:S(2)}, u32[]{:S(2)}) %all-to-all-start.1) | async-done | bytes 786464 | tf_op jit(solution)/shard_map/all_to_all | solution.py:405
  68.9 0.0 copy-done
  68.9 0.0 copy-start.1
  69.0 0.0 copy-start.2
  69.0 0.0 copy-start.3
  69.0 2.3 %forward_kernel.1 = (f32[256,768]{1,0:T(8,128)S(1)}, bf16[6,256,256]{2,1,0:T(8,128)(2,1)S(1)}, f32[256,768]{1,0:T(8,128)S(1)}, f32[256,768]{1,0:T(8,128)S(1)}, f32[8,256]{1,0:T(8,128)S(1)}) custom-call(s32[1]{0:T(128)} %bitcast.kept_ref, bf16[1,256,768]{2,1,0:T(8,128)(2,1)S(1)} %copy-done, bf16[512,768]{1,0:T(8,128)(2,1)S(1)} %bitcast.7, ...), custom_call_target="tpu_custom_call" | custom-call | tf_op jit(solution)/shard_map/forward_kernel/pallas_call | solution.py:301
  71.3 2.6 %collective-permute-start.2 = (f32[8,256]{1,0:T(8,128)S(1)}, f32[8,256]{1,0:T(8,128)S(1)}, u32[]{:S(2)}, u32[]{:S(2)}) collective-permute-start(f32[8,256]{1,0:T(8,128)S(1)} %get-tuple-element.27.stats0_ref), channel_id=1, source_target_pairs={{0,3},{1,0},{2,1},{3,2},{4,7},{5,4},{6,5},{7,6},{8,11},{9,8},{10,9... | collective-permute-start | bytes 24584 | tf_op jit(solution)/shard_map/ppermute | solution.py:426
  73.8 0.5 collective-permute-start.1
  74.3 0.6 collective-permute-start
  74.9 0.0 collective-permute-done.2.stats3_ref
  74.9 2.9 %collective-permute-done.1.stats2_ref = f32[8,256]{1,0:T(8,128)S(1)} collective-permute-done((f32[8,256]{1,0:T(8,128)S(1)}, f32[8,256]{1,0:T(8,128)S(1)}, u32[]{:S(2)}, u32[]{:S(2)}) %collective-permute-start.1) | collective-permute-done | bytes 8224 | tf_op jit(solution)/shard_map/ppermute | solution.py:426
  77.8 0.2 collective-permute-done.stats1_ref
  78.0 0.0 copy-done.1
  78.0 0.0 copy-done.2
  78.0 0.0 copy-done.3
  78.1 3.6 %score_grad_kernel.1 = (bf16[1,256,768]{2,1,0:T(8,128)(2,1)}, bf16[6,256,128]{2,1,0:T(8,128)(2,1)}, bf16[256,768]{1,0:T(8,128)(2,1)}, bf16[6,256,256]{2,1,0:T(8,...) custom-call(f32[8,256]{1,0:T(8,128)S(1)} %get-tuple-element.27.stats0_ref, ...), custom_call_target="tpu_custom_call" | custom-call | tf_op jit(solution)/shard_map/score_grad_kernel/pallas_call | solution.py:301
  81.7 7.9 %all-to-all-start.2 = ((bf16[64,8,128]{2,1,0:T(8,128)(2,1)}), bf16[64,8,128]{2,1,0:T(8,128)(2,1)S(1)}, u32[]{:S(2)}, u32[]{:S(2)}) async-start(bf16[64,8,128]{2,1,0:T(8,128)(2,1)} %get-tuple-element.41), calls=%async_computation.2 | async-start | bytes 262144 | tf_op jit(solution)/shard_map/all_to_all | solution.py:405
  89.6 3.2 %input_grad_kernel.1 = (bf16[1,256,768]{2,1,0:T(8,128)(2,1)}, bf16[1,256,768]{2,1,0:T(8,128)(2,1)}, bf16[1,256,768]{2,1,0:T(8,128)(2,1)}) custom-call(bf16[1,256,768]{2,1,0:T(8,128)(2,1)} %q_ref.5, bf16[1,256,768]{2,1,0:T(8,128)(2,1)} %ks_ref.3, bf16[256,768]{1,0:T(8,128)(2,1)} %get-tuple-element.34.mem_ref, ...), custom_call_target="tpu_custom_call" | custom-call | tf_op jit(solution)/shard_map/input_grad_kernel/pallas_call | solution.py:366
  92.8 7.1 %all-to-all-done.2.share_ref = bf16[64,8,128]{2,1,0:T(8,128)(2,1)S(1)} async-done(((bf16[64,8,128]{2,1,0:T(8,128)(2,1)}), bf16[64,8,128]{2,1,0:T(8,128)(2,1)S(1)}, u32[]{:S(2)}, u32[]{:S(2)}) %all-to-all-start.2) | async-done | bytes 131104 | tf_op jit(solution)/shard_map/all_to_all | solution.py:405
  99.9 0.9 collect.1
  (1 shorter events, 0.0 us)
Async XLA Ops:
  37.7 8.2 %copy-start.5 = (f32[768]{0:T(1024)S(1)}, f32[768]{0:T(1024)}, u32[]{:S(2)}) copy-start(f32[768]{0:T(1024)} %param.18) | copy-start | bytes 9220
  37.7 8.8 %copy-start.4 = (f32[6,512]{1,0:T(8,128)S(1)}, f32[6,512]{1,0:T(8,128)}, u32[]{:S(2)}) copy-start(f32[6,512]{1,0:T(8,128)} %param.17) | copy-start | bytes 36868
  39.6 11.7 %copy-start.6 = (s32[64]{0:T(128)S(1)}, s32[64]{0:T(128)}, u32[]{:S(2)}) copy-start(s32[64]{0:T(128)} %owner_ref.1) | copy-start | bytes 772
  39.6 11.7 %copy-start.7 = (s32[64]{0:T(128)S(1)}, s32[64]{0:T(128)}, u32[]{:S(2)}) copy-start(s32[64]{0:T(128)} %param.16) | copy-start | bytes 772
  39.6 29.3 %copy-start = (bf16[1,256,768]{2,1,0:T(8,128)(2,1)S(1)}, bf16[1,256,768]{2,1,0:T(8,128)(2,1)}, u32[]{:S(2)}) copy-start(bf16[1,256,768]{2,1,0:T(8,128)(2,1)} %q_ref.5) | copy-start | bytes 1179652
  39.6 29.3 %all-to-all-start.1 = ((bf16[64,8,768]{2,1,0:T(8,128)(2,1)}), bf16[64,8,768]{2,1,0:T(8,128)(2,1)S(1)}, u32[]{:S(2)}, u32[]{:S(2)}) async-start(bf16[64,8,768]{2,1,0:T(8,128)(2,1)} %reorder.1), calls=%async_computation.1 | async-start | bytes 1572864 | tf_op jit(solution)/shard_map/all_to_all | solution.py:405
  68.9 9.1 %copy-start.1 = (bf16[6,256,256]{2,1,0:T(8,128)(2,1)S(1)}, bf16[6,256,256]{2,1,0:T(8,128)(2,1)}, u32[]{:S(2)}) copy-start(bf16[6,256,256]{2,1,0:T(8,128)(2,1)} %get-tuple-element.30.prob_seg_ref) | copy-start | bytes 2359300
  69.0 9.1 %copy-start.2 = (bf16[1,256,768]{2,1,0:T(8,128)(2,1)S(1)}, bf16[1,256,768]{2,1,0:T(8,128)(2,1)}, u32[]{:S(2)}) copy-start(bf16[1,256,768]{2,1,0:T(8,128)(2,1)} %cot_ref.1) | copy-start | bytes 1179652
  69.0 9.1 %copy-start.3 = (f32[1,768]{1,0:T(1,128)S(1)}, f32[1,768]{1,0:T(1,128)}, u32[]{:S(2)}) copy-start(f32[1,768]{1,0:T(1,128)} %reshape.30.gain_ref) | copy-start | bytes 9220
  71.3 3.7 %collective-permute-start.2 = (f32[8,256]{1,0:T(8,128)S(1)}, f32[8,256]{1,0:T(8,128)S(1)}, u32[]{:S(2)}, u32[]{:S(2)}) collective-permute-start(f32[8,256]{1,0:T(8,128)S(1)} %get-tuple-element.27.stats0_ref), channel_id=1, source_target_pairs={{0,3},{1,0},{2,1},{3,2},{4,7},{5,4},{6,5},{7,6},{8,11},{9,8},{10,9... | collective-permute-start | bytes 24584 | tf_op jit(solution)/shard_map/ppermute | solution.py:426
  73.8 4.0 %collective-permute-start.1 = (f32[8,256]{1,0:T(8,128)S(1)}, f32[8,256]{1,0:T(8,128)S(1)}, u32[]{:S(2)}, u32[]{:S(2)}) collective-permute-start(f32[8,256]{1,0:T(8,128)S(1)} %get-tuple-element.27.stats0_ref), channel_id=1, source_target_pairs={{0,2},{1,3},{2,0},{3,1},{4,6},{5,7},{6,4},{7,5},{8,10},{9,11},{10,... | collective-permute-start | bytes 24584 | tf_op jit(solution)/shard_map/ppermute | solution.py:426
  74.3 3.7 %collective-permute-start = (f32[8,256]{1,0:T(8,128)S(1)}, f32[8,256]{1,0:T(8,128)S(1)}, u32[]{:S(2)}, u32[]{:S(2)}) collective-permute-start(f32[8,256]{1,0:T(8,128)S(1)} %get-tuple-element.27.stats0_ref), channel_id=1, source_target_pairs={{0,1},{1,2},{2,3},{3,0},{4,5},{5,6},{6,7},{7,4},{8,9},{9,10},{10,1... | collective-permute-start | bytes 24584 | tf_op jit(solution)/shard_map/ppermute | solution.py:426
  81.7 18.3 %all-to-all-start.2 = ((bf16[64,8,128]{2,1,0:T(8,128)(2,1)}), bf16[64,8,128]{2,1,0:T(8,128)(2,1)S(1)}, u32[]{:S(2)}, u32[]{:S(2)}) async-start(bf16[64,8,128]{2,1,0:T(8,128)(2,1)} %get-tuple-element.41), calls=%async_computation.2 | async-start | bytes 262144 | tf_op jit(solution)/shard_map/all_to_all | solution.py:405

commit v4 on v3

--- a/solution.py
+++ b/solution.py
@@ -112,7 +112,6 @@
     row = lax.broadcasted_iota(jnp.int32, (SEG, SEG), 0)
     lane = lax.broadcasted_iota(jnp.int32, (SEG, DH), 1)
     rows = jnp.zeros((SEG, DH), jnp.float32)
-    ones = jnp.ones((SEG, DH), jnp.bfloat16)
     table = by_distance(bias_ref[...] * LOG2E)
     for g in range(HEADS):
         cols = slice(DH * g, DH * g + DH)
@@ -123,14 +122,15 @@
         scores = dot(q_ref[0, :, cols], ks_ref[0, :, cols], NT) * FACTOR
         scores = jnp.where(col <= row, scores + bias[:, MEM:], -1e30)
         top = jnp.max(scores, axis=1, keepdims=True)
-        prob = jnp.exp2(scores - top).astype(jnp.bfloat16)
+        prob = jnp.exp2(scores - top)
+        total = jnp.sum(prob, axis=1, keepdims=True)
+        prob = (prob * (1.0 / total)).astype(jnp.bfloat16)
         prob_ref[g] = prob
-        both = dot(prob, jnp.concatenate([vs_ref[0, :, cols], ones], axis=1), NN)
-        out_ref[g] = both[:, :DH]
-        rows = jnp.where(lane == g, top, jnp.where(lane == 8 + g, both[:, DH:], rows))
-    table_ref[HALF * HEADS : HALF * HEADS + 16, :SEG] = rows.T[:16]
+        out_ref[g] = dot(prob, vs_ref[0, :, cols], NN).astype(jnp.bfloat16)
+        rows = jnp.where(lane == g, top + jnp.log2(total), rows)
+    table_ref[HALF * HEADS : HALF * HEADS + 8, :SEG] = rows.T[:8]
     for g in range(0, HEADS, 3):
-        row = HALF * HEADS + 16 + g // 3
+        row = HALF * HEADS + 8 + g // 3
         table_ref[row : row + 1] = gain_ref[:, DH * g : DH * g + 3 * DH]
 
 
@@ -146,7 +146,7 @@
     for copy in copies:
         copy.start()
     ones = jnp.ones((MEM, DH), jnp.bfloat16)
-    seg_row = table_ref[HALF * HEADS : HALF * HEADS + 16, :SEG]
+    seg_row = table_ref[HALF * HEADS : HALF * HEADS + 8, :SEG]
     both_kept = jnp.full((SEG, BLOCK), kept_ref[0], jnp.int32) > 1
     for g in range(HEADS):
         cols = slice(DH * g, DH * g + DH)
@@ -155,13 +155,12 @@
         scores = scores + jnp.concatenate([bias[:, DH:], bias[:, :MEM]], axis=0)
         scores = jnp.concatenate([jnp.where(both_kept, scores[:, :BLOCK], -1e30), scores[:, BLOCK:]], axis=1)
         seg_top = jnp.broadcast_to(seg_row[g : g + 1], (DH, SEG)).T
-        seg_total = jnp.broadcast_to(seg_row[8 + g : 9 + g], (DH, SEG)).T
         top = jnp.maximum(jnp.max(scores, axis=1, keepdims=True), seg_top)
         prob = jnp.exp2(scores - jnp.concatenate([top, top], axis=1)).astype(jnp.bfloat16)
         prob_ref[g] = prob
         both = dot(prob, jnp.concatenate([mem_ref[MEM:, cols], ones], axis=1), NN)
         shrink = jnp.exp2(seg_top - top)
-        inverse = 1.0 / (both[:, DH:] + seg_total * shrink)
+        inverse = 1.0 / (both[:, DH:] + shrink)
         factor_mem_ref[:, cols] = inverse
         factor_seg_ref[:, cols] = shrink * inverse
         out_ref[:, cols] = both[:, :DH] * inverse
@@ -170,9 +169,9 @@
     square = cross = None
     for g in range(HEADS):
         cols = slice(DH * g, DH * g + DH)
-        out = out_ref[:, cols] + seg_out_ref[g] * factor_seg_ref[:, cols]
+        out = out_ref[:, cols] + seg_out_ref[g].astype(jnp.float32) * factor_seg_ref[:, cols]
         out_ref[:, cols] = out
-        row = HALF * HEADS + 16 + g // 3
+        row = HALF * HEADS + 8 + g // 3
         gain = table_ref[row : row + 1, DH * (g % 3) : DH * (g % 3) + DH]
         part = cot_ref[:, cols].astype(jnp.float32) * gain * out
         square = out * out if g == 0 else square + out * out
@@ -272,7 +271,7 @@
 COLUMNS = jax.ShapeDtypeStruct((SEG, COLS), jnp.float32)
 HEAD_COLUMNS = jax.ShapeDtypeStruct((HEADS, SEG, DH), jnp.float32)
 HEAD_COLUMNS_B = jax.ShapeDtypeStruct((HEADS, SEG, DH), jnp.bfloat16)
-TABLE = jax.ShapeDtypeStruct((HEADS * HALF + 24, MEM + DH), jnp.float32)
+TABLE = jax.ShapeDtypeStruct((HEADS * HALF + 16, MEM + DH), jnp.float32)
 STATS = jax.ShapeDtypeStruct((8, SEG), jnp.float32)
 KEYS = jax.ShapeDtypeStruct((MEM, COLS), jnp.bfloat16)
 SHARES = jax.ShapeDtypeStruct((DP, 8, DH), jnp.bfloat16)
@@ -317,7 +316,7 @@
         segment_kernel,
         in_specs=[spec] * 5,
         out_shape=(
-            far_out(SQUARES_B), far_out(HEAD_COLUMNS), near_out(TABLE),
+            far_out(SQUARES_B), far_out(HEAD_COLUMNS_B), near_out(TABLE),
         ),
         out_specs=(spec,) * 3,
         compiler_params=pltpu.CompilerParams(vmem_limit_bytes=LIMIT << 20),
@@ -334,7 +333,7 @@
         [near_out(x) for x in (COLUMNS, SQUARES_B, COLUMNS, COLUMNS, STATS)],
         (),
         scratch=[
-            pltpu.VMEM((HEADS, SEG, DH), jnp.float32),
+            pltpu.VMEM((HEADS, SEG, DH), jnp.bfloat16),
             pltpu.VMEM((SEG, COLS), jnp.bfloat16),
             pltpu.SemaphoreType.DMA((2,)),
         ],

time: 101 us -> 101 us (level)
  transfers between devices with their start and end apart: 5 -> 5, of which waited for: 4 -> 4; matrix products, arithmetic and copies ran while one was open for 1% -> 1% of each run, Pallas kernels for 8% -> 7%
where the time goes in v4:
time: 101 us
  blocking collectives  35.9 us (36%)
  waiting for transfers between devices  27.7 us (27%)
  starting transfers between devices  17.9 us (18%)
  Pallas kernels  16 us (16%)
  other arithmetic  1.8 us (2%)
    all_to_all x1, blocking collectives, exchange(): return lax.all_to_all(x, 'dp', split_axis=0, concat_axis=0, tiled=True)  35.9 us
    all_to_all x2, waiting for transfers between devices, exchange(): return lax.all_to_all(x, 'dp', split_axis=0, concat_axis=0, tiled=True)  24.6 us
    all_to_all x2, starting transfers between devices, exchange(): return lax.all_to_all(x, 'dp', split_axis=0, concat_axis=0, tiled=True)  14.3 us
    pallas_call x2, Pallas kernels, near_call(): pl.pallas_call(kernel, in_specs=[pl.BlockSpec(memory_space=pltpu.SMEM)] *...  5.79 us
    pallas_call x1, Pallas kernels, segment(): pl.pallas_call(segment_kernel, in_specs=[spec] * 5, out_shape=(far_out(SQ...  4.33 us
    ppermute x3, starting transfers between devices, body(): lax.ppermute(stats, 'mp', [(i, (i + step) % 4) for i in range(4)])  3.68 us
    pallas_call x1, Pallas kernels, input_grad(): pl.pallas_call(input_grad_kernel, grid=(HEADS // GROUP,), in_specs=[token...  3.22 us
    ppermute x3, waiting for transfers between devices, body(): lax.ppermute(stats, 'mp', [(i, (i + step) % 4) for i in range(4)])  3.1 us
  transfers between devices with their start and end apart: 5, of which 4 were waited for; matrix products, arithmetic and copies ran while one was open for 1% of the time, Pallas kernels for 7%

profile of v4, /device:TPU:1, one launch (start us, length us, event | category | flops | bytes accessed | tf_op | source)
XLA Modules:
  0.0 100.7 jit_solution(12025284204178031191)
XLA Ops:
  0.6 1.2 %maximum_bitcast_fusion = bf16[64,8,768]{2,1,0:T(8,128)(2,1)S(1)} fusion(bf16[256,768]{1,0:T(8,128)(2,1)} %bitcast.9, bf16[256,768]{1,0:T(8,128)(2,1)} %bitcast.10), kind=kLoop, calls=%fused_computation | loop fusion | flops 1572864 | bytes 1572864 | tf_op jit(solution)/shard_map/reshape | solution.py:415
  1.8 35.9 %all_to_all.15.in_ref = bf16[64,8,768]{2,1,0:T(8,128)(2,1)S(1)} all-to-all(bf16[64,8,768]{2,1,0:T(8,128)(2,1)S(1)} %maximum_bitcast_fusion), channel_id=1, replica_groups=mesh['dp'=64,'mp'=4] {'dp'}, dimensions={0} | all-to-all | bytes 1572864 | tf_op jit(solution)/shard_map/all_to_all | solution.py:404
  37.7 0.0 copy-start.5
  37.7 0.0 copy-start.4
  37.7 1.8 %reorder.1 = bf16[64,8,768]{2,1,0:T(8,128)(2,1)} custom-call(s32[64]{0:T(128)} %owner_ref.1, bf16[64,8,768]{2,1,0:T(8,128)(2,1)S(1)} %all_to_all.15.in_ref), custom_call_target="tpu_custom_call" | custom-call | tf_op jit(solution)/shard_map/reorder/pallas_call | solution.py:91
  39.6 0.0 copy-start.6
  39.6 0.0 copy-start.7
  39.6 0.0 copy-start
  39.6 6.3 %all-to-all-start.1 = ((bf16[64,8,768]{2,1,0:T(8,128)(2,1)}), bf16[64,8,768]{2,1,0:T(8,128)(2,1)S(1)}, u32[]{:S(2)}, u32[]{:S(2)}) async-start(bf16[64,8,768]{2,1,0:T(8,128)(2,1)} %reorder.1), calls=%async_computation.1 | async-start | bytes 1572864 | tf_op jit(solution)/shard_map/all_to_all | solution.py:404
  46.0 0.0 copy-done.5
  46.0 0.6 reshape.30.gain_ref
  46.6 0.0 copy-done.4
  46.6 4.3 %segment_kernel.1 = (bf16[6,256,256]{2,1,0:T(8,128)(2,1)}, bf16[6,256,128]{2,1,0:T(8,128)(2,1)}, f32[784,384]{1,0:T(8,128)S(1)}) custom-call(bf16[1,256,768]{2,1,0:T(8,128)(2,1)} %q_ref.5, bf16[1,256,768]{2,1,0:T(8,128)(2,1)} %ks_ref.3, bf16[1,256,768]{2,1,0:T(8,128)(2,1)} %vs_hbm.1, f32[8,512]{1,0:T(8,128)S(1)} %pad.4.bias_ref, f32[1,768]{1,0:T(1,128)} %reshape.30.gain_ref), custom_call_target="tpu_custom_call" | custom-call | tf_op jit(solution)/shard_map/segment_kernel/pallas_call | solution.py:315
  50.9 0.0 copy-done.6
  50.9 0.0 copy-done.7
  50.9 0.6 fusion
  51.5 17.4 %all-to-all-done.1 = bf16[64,8,768]{2,1,0:T(8,128)(2,1)S(1)} async-done(((bf16[64,8,768]{2,1,0:T(8,128)(2,1)}), bf16[64,8,768]{2,1,0:T(8,128)(2,1)S(1)}, u32[]{:S(2)}, u32[]{:S(2)}) %all-to-all-start.1) | async-done | bytes 786464 | tf_op jit(solution)/shard_map/all_to_all | solution.py:404
  68.9 0.0 copy-done
  68.9 0.0 copy-start.1
  69.0 0.0 copy-start.2
  69.0 0.0 copy-start.3
  69.0 2.2 %forward_kernel.1 = (f32[256,768]{1,0:T(8,128)S(1)}, bf16[6,256,256]{2,1,0:T(8,128)(2,1)S(1)}, f32[256,768]{1,0:T(8,128)S(1)}, f32[256,768]{1,0:T(8,128)S(1)}, f32[8,256]{1,0:T(8,128)S(1)}) custom-call(s32[1]{0:T(128)} %bitcast.kept_ref, bf16[1,256,768]{2,1,0:T(8,128)(2,1)S(1)} %copy-done, bf16[512,768]{1,0:T(8,128)(2,1)S(1)} %bitcast.7, ...), custom_call_target="tpu_custom_call" | custom-call | tf_op jit(solution)/shard_map/forward_kernel/pallas_call | solution.py:300
  71.2 2.6 %collective-permute-start.2 = (f32[8,256]{1,0:T(8,128)S(1)}, f32[8,256]{1,0:T(8,128)S(1)}, u32[]{:S(2)}, u32[]{:S(2)}) collective-permute-start(f32[8,256]{1,0:T(8,128)S(1)} %get-tuple-element.27.stats0_ref), channel_id=1, source_target_pairs={{0,3},{1,0},{2,1},{3,2},{4,7},{5,4},{6,5},{7,6},{8,11},{9,8},{10,9... | collective-permute-start | bytes 24584 | tf_op jit(solution)/shard_map/ppermute | solution.py:425
  73.7 0.5 collective-permute-start.1
  74.2 0.6 collective-permute-start
  74.8 0.0 collective-permute-done.2.stats3_ref
  74.8 2.9 %collective-permute-done.1.stats2_ref = f32[8,256]{1,0:T(8,128)S(1)} collective-permute-done((f32[8,256]{1,0:T(8,128)S(1)}, f32[8,256]{1,0:T(8,128)S(1)}, u32[]{:S(2)}, u32[]{:S(2)}) %collective-permute-start.1) | collective-permute-done | bytes 8224 | tf_op jit(solution)/shard_map/ppermute | solution.py:425
  77.7 0.2 collective-permute-done.stats1_ref
  77.9 0.0 copy-done.1
  77.9 0.0 copy-done.2
  77.9 0.0 copy-done.3
  78.0 3.6 %score_grad_kernel.1 = (bf16[1,256,768]{2,1,0:T(8,128)(2,1)}, bf16[6,256,128]{2,1,0:T(8,128)(2,1)}, bf16[256,768]{1,0:T(8,128)(2,1)}, bf16[6,256,256]{2,1,0:T(8,...) custom-call(f32[8,256]{1,0:T(8,128)S(1)} %get-tuple-element.27.stats0_ref, ...), custom_call_target="tpu_custom_call" | custom-call | tf_op jit(solution)/shard_map/score_grad_kernel/pallas_call | solution.py:300
  81.6 7.9 %all-to-all-start.2 = ((bf16[64,8,128]{2,1,0:T(8,128)(2,1)}), bf16[64,8,128]{2,1,0:T(8,128)(2,1)S(1)}, u32[]{:S(2)}, u32[]{:S(2)}) async-start(bf16[64,8,128]{2,1,0:T(8,128)(2,1)} %get-tuple-element.41), calls=%async_computation.2 | async-start | bytes 262144 | tf_op jit(solution)/shard_map/all_to_all | solution.py:404
  89.5 3.2 %input_grad_kernel.1 = (bf16[1,256,768]{2,1,0:T(8,128)(2,1)}, bf16[1,256,768]{2,1,0:T(8,128)(2,1)}, bf16[1,256,768]{2,1,0:T(8,128)(2,1)}) custom-call(bf16[1,256,768]{2,1,0:T(8,128)(2,1)} %q_ref.5, bf16[1,256,768]{2,1,0:T(8,128)(2,1)} %ks_ref.3, bf16[256,768]{1,0:T(8,128)(2,1)} %get-tuple-element.34.mem_ref, ...), custom_call_target="tpu_custom_call" | custom-call | tf_op jit(solution)/shard_map/input_grad_kernel/pallas_call | solution.py:365
  92.7 7.1 %all-to-all-done.2.share_ref = bf16[64,8,128]{2,1,0:T(8,128)(2,1)S(1)} async-done(((bf16[64,8,128]{2,1,0:T(8,128)(2,1)}), bf16[64,8,128]{2,1,0:T(8,128)(2,1)S(1)}, u32[]{:S(2)}, u32[]{:S(2)}) %all-to-all-start.2) | async-done | bytes 131104 | tf_op jit(solution)/shard_map/all_to_all | solution.py:404
  99.9 0.9 collect.1
  (1 shorter events, 0.0 us)
Async XLA Ops:
  37.7 8.2 %copy-start.5 = (f32[768]{0:T(1024)S(1)}, f32[768]{0:T(1024)}, u32[]{:S(2)}) copy-start(f32[768]{0:T(1024)} %param.18) | copy-start | bytes 9220
  37.7 8.8 %copy-start.4 = (f32[6,512]{1,0:T(8,128)S(1)}, f32[6,512]{1,0:T(8,128)}, u32[]{:S(2)}) copy-start(f32[6,512]{1,0:T(8,128)} %param.17) | copy-start | bytes 36868
  39.6 11.3 %copy-start.6 = (s32[64]{0:T(128)S(1)}, s32[64]{0:T(128)}, u32[]{:S(2)}) copy-start(s32[64]{0:T(128)} %owner_ref.1) | copy-start | bytes 772
  39.6 11.3 %copy-start.7 = (s32[64]{0:T(128)S(1)}, s32[64]{0:T(128)}, u32[]{:S(2)}) copy-start(s32[64]{0:T(128)} %param.16) | copy-start | bytes 772
  39.6 29.3 %copy-start = (bf16[1,256,768]{2,1,0:T(8,128)(2,1)S(1)}, bf16[1,256,768]{2,1,0:T(8,128)(2,1)}, u32[]{:S(2)}) copy-start(bf16[1,256,768]{2,1,0:T(8,128)(2,1)} %q_ref.5) | copy-start | bytes 1179652
  39.6 29.3 %all-to-all-start.1 = ((bf16[64,8,768]{2,1,0:T(8,128)(2,1)}), bf16[64,8,768]{2,1,0:T(8,128)(2,1)S(1)}, u32[]{:S(2)}, u32[]{:S(2)}) async-start(bf16[64,8,768]{2,1,0:T(8,128)(2,1)} %reorder.1), calls=%async_computation.1 | async-start | bytes 1572864 | tf_op jit(solution)/shard_map/all_to_all | solution.py:404
  68.9 9.0 %copy-start.1 = (bf16[6,256,256]{2,1,0:T(8,128)(2,1)S(1)}, bf16[6,256,256]{2,1,0:T(8,128)(2,1)}, u32[]{:S(2)}) copy-start(bf16[6,256,256]{2,1,0:T(8,128)(2,1)} %get-tuple-element.30.prob_seg_ref) | copy-start | bytes 2359300
  69.0 9.0 %copy-start.2 = (bf16[1,256,768]{2,1,0:T(8,128)(2,1)S(1)}, bf16[1,256,768]{2,1,0:T(8,128)(2,1)}, u32[]{:S(2)}) copy-start(bf16[1,256,768]{2,1,0:T(8,128)(2,1)} %cot_ref.1) | copy-start | bytes 1179652
  69.0 9.0 %copy-start.3 = (f32[1,768]{1,0:T(1,128)S(1)}, f32[1,768]{1,0:T(1,128)}, u32[]{:S(2)}) copy-start(f32[1,768]{1,0:T(1,128)} %reshape.30.gain_ref) | copy-start | bytes 9220
  71.2 3.7 %collective-permute-start.2 = (f32[8,256]{1,0:T(8,128)S(1)}, f32[8,256]{1,0:T(8,128)S(1)}, u32[]{:S(2)}, u32[]{:S(2)}) collective-permute-start(f32[8,256]{1,0:T(8,128)S(1)} %get-tuple-element.27.stats0_ref), channel_id=1, source_target_pairs={{0,3},{1,0},{2,1},{3,2},{4,7},{5,4},{6,5},{7,6},{8,11},{9,8},{10,9... | collective-permute-start | bytes 24584 | tf_op jit(solution)/shard_map/ppermute | solution.py:425
  73.7 4.0 %collective-permute-start.1 = (f32[8,256]{1,0:T(8,128)S(1)}, f32[8,256]{1,0:T(8,128)S(1)}, u32[]{:S(2)}, u32[]{:S(2)}) collective-permute-start(f32[8,256]{1,0:T(8,128)S(1)} %get-tuple-element.27.stats0_ref), channel_id=1, source_target_pairs={{0,2},{1,3},{2,0},{3,1},{4,6},{5,7},{6,4},{7,5},{8,10},{9,11},{10,... | collective-permute-start | bytes 24584 | tf_op jit(solution)/shard_map/ppermute | solution.py:425
  74.2 3.7 %collective-permute-start = (f32[8,256]{1,0:T(8,128)S(1)}, f32[8,256]{1,0:T(8,128)S(1)}, u32[]{:S(2)}, u32[]{:S(2)}) collective-permute-start(f32[8,256]{1,0:T(8,128)S(1)} %get-tuple-element.27.stats0_ref), channel_id=1, source_target_pairs={{0,1},{1,2},{2,3},{3,0},{4,5},{5,6},{6,7},{7,4},{8,9},{9,10},{10,1... | collective-permute-start | bytes 24584 | tf_op jit(solution)/shard_map/ppermute | solution.py:425
  81.6 18.3 %all-to-all-start.2 = ((bf16[64,8,128]{2,1,0:T(8,128)(2,1)}), bf16[64,8,128]{2,1,0:T(8,128)(2,1)S(1)}, u32[]{:S(2)}, u32[]{:S(2)}) async-start(bf16[64,8,128]{2,1,0:T(8,128)(2,1)} %get-tuple-element.41), calls=%async_computation.2 | async-start | bytes 262144 | tf_op jit(solution)/shard_map/all_to_all | solution.py:404

commit v5 on v4

--- a/solution.py
+++ b/solution.py
@@ -22,7 +22,7 @@
 SCALE = DH ** (-0.5)
 FACTOR = SCALE * LOG2E
 GROUP = 3
-CHUNK = 16
+CHUNK = 32
 LIMIT = 16
 NT = (((1,), (1,)), ((), ()))
 NN = (((1,), (0,)), ((), ()))
@@ -126,7 +126,7 @@
         total = jnp.sum(prob, axis=1, keepdims=True)
         prob = (prob * (1.0 / total)).astype(jnp.bfloat16)
         prob_ref[g] = prob
-        out_ref[g] = dot(prob, vs_ref[0, :, cols], NN).astype(jnp.bfloat16)
+        out_ref[g] = dot(prob, vs_ref[0, :, cols], NN)
         rows = jnp.where(lane == g, top + jnp.log2(total), rows)
     table_ref[HALF * HEADS : HALF * HEADS + 8, :SEG] = rows.T[:8]
     for g in range(0, HEADS, 3):
@@ -169,7 +169,7 @@
     square = cross = None
     for g in range(HEADS):
         cols = slice(DH * g, DH * g + DH)
-        out = out_ref[:, cols] + seg_out_ref[g].astype(jnp.float32) * factor_seg_ref[:, cols]
+        out = out_ref[:, cols] + seg_out_ref[g] * factor_seg_ref[:, cols]
         out_ref[:, cols] = out
         row = HALF * HEADS + 8 + g // 3
         gain = table_ref[row : row + 1, DH * (g % 3) : DH * (g % 3) + DH]
@@ -316,7 +316,7 @@
         segment_kernel,
         in_specs=[spec] * 5,
         out_shape=(
-            far_out(SQUARES_B), far_out(HEAD_COLUMNS_B), near_out(TABLE),
+            far_out(SQUARES_B), far_out(HEAD_COLUMNS), near_out(TABLE),
         ),
         out_specs=(spec,) * 3,
         compiler_params=pltpu.CompilerParams(vmem_limit_bytes=LIMIT << 20),
@@ -333,7 +333,7 @@
         [near_out(x) for x in (COLUMNS, SQUARES_B, COLUMNS, COLUMNS, STATS)],
         (),
         scratch=[
-            pltpu.VMEM((HEADS, SEG, DH), jnp.bfloat16),
+            pltpu.VMEM((HEADS, SEG, DH), jnp.float32),
             pltpu.VMEM((SEG, COLS), jnp.bfloat16),
             pltpu.SemaphoreType.DMA((2,)),
         ],

time: 101 us -> 101 us (level)
  transfers between devices with their start and end apart: 5 -> 5, of which waited for: 4 -> 4; matrix products, arithmetic and copies ran while one was open for 1% -> 1% of each run, Pallas kernels for 7% -> 8%
where the time goes in v5:
time: 101 us
  blocking collectives  35.9 us (36%)
  waiting for transfers between devices  27.5 us (27%)
  starting transfers between devices  17.9 us (18%)
  Pallas kernels  16.3 us (16%)
  other arithmetic  1.8 us (2%)
    all_to_all x1, blocking collectives, exchange(): return lax.all_to_all(x, 'dp', split_axis=0, concat_axis=0, tiled=True)  35.9 us
    all_to_all x2, waiting for transfers between devices, exchange(): return lax.all_to_all(x, 'dp', split_axis=0, concat_axis=0, tiled=True)  24.4 us
    all_to_all x2, starting transfers between devices, exchange(): return lax.all_to_all(x, 'dp', split_axis=0, concat_axis=0, tiled=True)  14.2 us
    pallas_call x2, Pallas kernels, near_call(): pl.pallas_call(kernel, in_specs=[pl.BlockSpec(memory_space=pltpu.SMEM)] *...  5.89 us
    pallas_call x1, Pallas kernels, segment(): pl.pallas_call(segment_kernel, in_specs=[spec] * 5, out_shape=(far_out(SQ...  4.47 us
    ppermute x3, starting transfers between devices, body(): lax.ppermute(stats, 'mp', [(i, (i + step) % 4) for i in range(4)])  3.68 us
    pallas_call x1, Pallas kernels, input_grad(): pl.pallas_call(input_grad_kernel, grid=(HEADS // GROUP,), in_specs=[token...  3.22 us
    ppermute x3, waiting for transfers between devices, body(): lax.ppermute(stats, 'mp', [(i, (i + step) % 4) for i in range(4)])  3.1 us
  transfers between devices with their start and end apart: 5, of which 4 were waited for; matrix products, arithmetic and copies ran while one was open for 1% of the time, Pallas kernels for 8%

profile of v5, /device:TPU:1, one launch (start us, length us, event | category | flops | bytes accessed | tf_op | source)
XLA Modules:
  0.0 100.8 jit_solution(7503312528384907282)
XLA Ops:
  0.6 1.2 %maximum_bitcast_fusion = bf16[64,8,768]{2,1,0:T(8,128)(2,1)S(1)} fusion(bf16[256,768]{1,0:T(8,128)(2,1)} %bitcast.9, bf16[256,768]{1,0:T(8,128)(2,1)} %bitcast.10), kind=kLoop, calls=%fused_computation | loop fusion | flops 1572864 | bytes 1572864 | tf_op jit(solution)/shard_map/reshape | solution.py:415
  1.8 35.9 %all_to_all.15.in_ref = bf16[64,8,768]{2,1,0:T(8,128)(2,1)S(1)} all-to-all(bf16[64,8,768]{2,1,0:T(8,128)(2,1)S(1)} %maximum_bitcast_fusion), channel_id=1, replica_groups=mesh['dp'=64,'mp'=4] {'dp'}, dimensions={0} | all-to-all | bytes 1572864 | tf_op jit(solution)/shard_map/all_to_all | solution.py:404
  37.7 0.0 copy-start.5
  37.7 0.0 copy-start.4
  37.7 1.8 %reorder.1 = bf16[64,8,768]{2,1,0:T(8,128)(2,1)} custom-call(s32[64]{0:T(128)} %owner_ref.1, bf16[64,8,768]{2,1,0:T(8,128)(2,1)S(1)} %all_to_all.15.in_ref), custom_call_target="tpu_custom_call" | custom-call | tf_op jit(solution)/shard_map/reorder/pallas_call | solution.py:91
  39.6 0.0 copy-start.6
  39.6 0.0 copy-start.7
  39.6 0.0 copy-start
  39.6 6.3 %all-to-all-start.1 = ((bf16[64,8,768]{2,1,0:T(8,128)(2,1)}), bf16[64,8,768]{2,1,0:T(8,128)(2,1)S(1)}, u32[]{:S(2)}, u32[]{:S(2)}) async-start(bf16[64,8,768]{2,1,0:T(8,128)(2,1)} %reorder.1), calls=%async_computation.1 | async-start | bytes 1572864 | tf_op jit(solution)/shard_map/all_to_all | solution.py:404
  46.0 0.0 copy-done.5
  46.0 0.6 reshape.30.gain_ref
  46.6 0.0 copy-done.4
  46.6 4.5 %segment_kernel.1 = (bf16[6,256,256]{2,1,0:T(8,128)(2,1)}, f32[6,256,128]{2,1,0:T(8,128)}, f32[784,384]{1,0:T(8,128)S(1)}) custom-call(bf16[1,256,768]{2,1,0:T(8,128)(2,1)} %q_ref.5, bf16[1,256,768]{2,1,0:T(8,128)(2,1)} %ks_ref.3, bf16[1,256,768]{2,1,0:T(8,128)(2,1)} %vs_hbm.1, f32[8,512]{1,0:T(8,128)S(1)} %pad.4.bias_ref, f32[1,768]{1,0:T(1,128)} %reshape.30.gain_ref), custom_call_target="tpu_custom_call" | custom-call | tf_op jit(solution)/shard_map/segment_kernel/pallas_call | solution.py:315
  51.0 0.0 copy-done.6
  51.0 0.0 copy-done.7
  51.0 0.6 fusion
  51.7 17.3 %all-to-all-done.1 = bf16[64,8,768]{2,1,0:T(8,128)(2,1)S(1)} async-done(((bf16[64,8,768]{2,1,0:T(8,128)(2,1)}), bf16[64,8,768]{2,1,0:T(8,128)(2,1)S(1)}, u32[]{:S(2)}, u32[]{:S(2)}) %all-to-all-start.1) | async-done | bytes 786464 | tf_op jit(solution)/shard_map/all_to_all | solution.py:404
  68.9 0.0 copy-done
  68.9 0.0 copy-start.1
  68.9 0.0 copy-start.2
  68.9 0.0 copy-start.3
  69.0 2.3 %forward_kernel.1 = (f32[256,768]{1,0:T(8,128)S(1)}, bf16[6,256,256]{2,1,0:T(8,128)(2,1)S(1)}, f32[256,768]{1,0:T(8,128)S(1)}, f32[256,768]{1,0:T(8,128)S(1)}, f32[8,256]{1,0:T(8,128)S(1)}) custom-call(s32[1]{0:T(128)} %bitcast.kept_ref, bf16[1,256,768]{2,1,0:T(8,128)(2,1)S(1)} %copy-done, bf16[512,768]{1,0:T(8,128)(2,1)S(1)} %bitcast.7, ...), custom_call_target="tpu_custom_call" | custom-call | tf_op jit(solution)/shard_map/forward_kernel/pallas_call | solution.py:300
  71.3 2.6 %collective-permute-start.2 = (f32[8,256]{1,0:T(8,128)S(1)}, f32[8,256]{1,0:T(8,128)S(1)}, u32[]{:S(2)}, u32[]{:S(2)}) collective-permute-start(f32[8,256]{1,0:T(8,128)S(1)} %get-tuple-element.27.stats0_ref), channel_id=1, source_target_pairs={{0,3},{1,0},{2,1},{3,2},{4,7},{5,4},{6,5},{7,6},{8,11},{9,8},{10,9... | collective-permute-start | bytes 24584 | tf_op jit(solution)/shard_map/ppermute | solution.py:425
  73.8 0.5 collective-permute-start.1
  74.3 0.6 collective-permute-start
  74.9 0.0 collective-permute-done.2.stats3_ref
  74.9 2.9 %collective-permute-done.1.stats2_ref = f32[8,256]{1,0:T(8,128)S(1)} collective-permute-done((f32[8,256]{1,0:T(8,128)S(1)}, f32[8,256]{1,0:T(8,128)S(1)}, u32[]{:S(2)}, u32[]{:S(2)}) %collective-permute-start.1) | collective-permute-done | bytes 8224 | tf_op jit(solution)/shard_map/ppermute | solution.py:425
  77.8 0.2 collective-permute-done.stats1_ref
  78.0 0.0 copy-done.1
  78.0 0.0 copy-done.2
  78.0 0.0 copy-done.3
  78.1 3.6 %score_grad_kernel.1 = (bf16[1,256,768]{2,1,0:T(8,128)(2,1)}, bf16[6,256,128]{2,1,0:T(8,128)(2,1)}, bf16[256,768]{1,0:T(8,128)(2,1)}, bf16[6,256,256]{2,1,0:T(8,...) custom-call(f32[8,256]{1,0:T(8,128)S(1)} %get-tuple-element.27.stats0_ref, ...), custom_call_target="tpu_custom_call" | custom-call | tf_op jit(solution)/shard_map/score_grad_kernel/pallas_call | solution.py:300
  81.7 7.9 %all-to-all-start.2 = ((bf16[64,8,128]{2,1,0:T(8,128)(2,1)}), bf16[64,8,128]{2,1,0:T(8,128)(2,1)S(1)}, u32[]{:S(2)}, u32[]{:S(2)}) async-start(bf16[64,8,128]{2,1,0:T(8,128)(2,1)} %get-tuple-element.41), calls=%async_computation.2 | async-start | bytes 262144 | tf_op jit(solution)/shard_map/all_to_all | solution.py:404
  89.6 3.2 %input_grad_kernel.1 = (bf16[1,256,768]{2,1,0:T(8,128)(2,1)}, bf16[1,256,768]{2,1,0:T(8,128)(2,1)}, bf16[1,256,768]{2,1,0:T(8,128)(2,1)}) custom-call(bf16[1,256,768]{2,1,0:T(8,128)(2,1)} %q_ref.5, bf16[1,256,768]{2,1,0:T(8,128)(2,1)} %ks_ref.3, bf16[256,768]{1,0:T(8,128)(2,1)} %get-tuple-element.34.mem_ref, ...), custom_call_target="tpu_custom_call" | custom-call | tf_op jit(solution)/shard_map/input_grad_kernel/pallas_call | solution.py:365
  92.8 7.1 %all-to-all-done.2.share_ref = bf16[64,8,128]{2,1,0:T(8,128)(2,1)S(1)} async-done(((bf16[64,8,128]{2,1,0:T(8,128)(2,1)}), bf16[64,8,128]{2,1,0:T(8,128)(2,1)S(1)}, u32[]{:S(2)}, u32[]{:S(2)}) %all-to-all-start.2) | async-done | bytes 131104 | tf_op jit(solution)/shard_map/all_to_all | solution.py:404
  99.9 0.9 collect.1
  (1 shorter events, 0.0 us)
Async XLA Ops:
  37.7 8.2 %copy-start.5 = (f32[768]{0:T(1024)S(1)}, f32[768]{0:T(1024)}, u32[]{:S(2)}) copy-start(f32[768]{0:T(1024)} %param.18) | copy-start | bytes 9220
  37.7 8.8 %copy-start.4 = (f32[6,512]{1,0:T(8,128)S(1)}, f32[6,512]{1,0:T(8,128)}, u32[]{:S(2)}) copy-start(f32[6,512]{1,0:T(8,128)} %param.17) | copy-start | bytes 36868
  39.6 11.5 %copy-start.6 = (s32[64]{0:T(128)S(1)}, s32[64]{0:T(128)}, u32[]{:S(2)}) copy-start(s32[64]{0:T(128)} %owner_ref.1) | copy-start | bytes 772
  39.6 11.4 %copy-start.7 = (s32[64]{0:T(128)S(1)}, s32[64]{0:T(128)}, u32[]{:S(2)}) copy-start(s32[64]{0:T(128)} %param.16) | copy-start | bytes 772
  39.6 29.3 %copy-start = (bf16[1,256,768]{2,1,0:T(8,128)(2,1)S(1)}, bf16[1,256,768]{2,1,0:T(8,128)(2,1)}, u32[]{:S(2)}) copy-start(bf16[1,256,768]{2,1,0:T(8,128)(2,1)} %q_ref.5) | copy-start | bytes 1179652
  39.6 29.3 %all-to-all-start.1 = ((bf16[64,8,768]{2,1,0:T(8,128)(2,1)}), bf16[64,8,768]{2,1,0:T(8,128)(2,1)S(1)}, u32[]{:S(2)}, u32[]{:S(2)}) async-start(bf16[64,8,768]{2,1,0:T(8,128)(2,1)} %reorder.1), calls=%async_computation.1 | async-start | bytes 1572864 | tf_op jit(solution)/shard_map/all_to_all | solution.py:404
  68.9 9.1 %copy-start.1 = (bf16[6,256,256]{2,1,0:T(8,128)(2,1)S(1)}, bf16[6,256,256]{2,1,0:T(8,128)(2,1)}, u32[]{:S(2)}) copy-start(bf16[6,256,256]{2,1,0:T(8,128)(2,1)} %get-tuple-element.30.prob_seg_ref) | copy-start | bytes 2359300
  68.9 9.1 %copy-start.2 = (bf16[1,256,768]{2,1,0:T(8,128)(2,1)S(1)}, bf16[1,256,768]{2,1,0:T(8,128)(2,1)}, u32[]{:S(2)}) copy-start(bf16[1,256,768]{2,1,0:T(8,128)(2,1)} %cot_ref.1) | copy-start | bytes 1179652
  68.9 9.1 %copy-start.3 = (f32[1,768]{1,0:T(1,128)S(1)}, f32[1,768]{1,0:T(1,128)}, u32[]{:S(2)}) copy-start(f32[1,768]{1,0:T(1,128)} %reshape.30.gain_ref) | copy-start | bytes 9220
  71.3 3.7 %collective-permute-start.2 = (f32[8,256]{1,0:T(8,128)S(1)}, f32[8,256]{1,0:T(8,128)S(1)}, u32[]{:S(2)}, u32[]{:S(2)}) collective-permute-start(f32[8,256]{1,0:T(8,128)S(1)} %get-tuple-element.27.stats0_ref), channel_id=1, source_target_pairs={{0,3},{1,0},{2,1},{3,2},{4,7},{5,4},{6,5},{7,6},{8,11},{9,8},{10,9... | collective-permute-start | bytes 24584 | tf_op jit(solution)/shard_map/ppermute | solution.py:425
  73.8 4.0 %collective-permute-start.1 = (f32[8,256]{1,0:T(8,128)S(1)}, f32[8,256]{1,0:T(8,128)S(1)}, u32[]{:S(2)}, u32[]{:S(2)}) collective-permute-start(f32[8,256]{1,0:T(8,128)S(1)} %get-tuple-element.27.stats0_ref), channel_id=1, source_target_pairs={{0,2},{1,3},{2,0},{3,1},{4,6},{5,7},{6,4},{7,5},{8,10},{9,11},{10,... | collective-permute-start | bytes 24584 | tf_op jit(solution)/shard_map/ppermute | solution.py:425
  74.3 3.7 %collective-permute-start = (f32[8,256]{1,0:T(8,128)S(1)}, f32[8,256]{1,0:T(8,128)S(1)}, u32[]{:S(2)}, u32[]{:S(2)}) collective-permute-start(f32[8,256]{1,0:T(8,128)S(1)} %get-tuple-element.27.stats0_ref), channel_id=1, source_target_pairs={{0,1},{1,2},{2,3},{3,0},{4,5},{5,6},{6,7},{7,4},{8,9},{9,10},{10,1... | collective-permute-start | bytes 24584 | tf_op jit(solution)/shard_map/ppermute | solution.py:425
  81.7 18.3 %all-to-all-start.2 = ((bf16[64,8,128]{2,1,0:T(8,128)(2,1)}), bf16[64,8,128]{2,1,0:T(8,128)(2,1)S(1)}, u32[]{:S(2)}, u32[]{:S(2)}) async-start(bf16[64,8,128]{2,1,0:T(8,128)(2,1)} %get-tuple-element.41), calls=%async_computation.2 | async-start | bytes 262144 | tf_op jit(solution)/shard_map/all_to_all | solution.py:404
